TPU v7x, 256 devices: a whole 4x4x8 slice. The times are simulated.
256 devices in a mesh: dp: 32 (over y, z_lo, core), seq: 8 (over z_hi, x).
Axes of the slice: x: 4, y: 4, z: 8 (z_hi: 2, z_lo: 4; z = z_hi * 4 + z_lo), core: 2. Of those that a mesh axis runs over, the one named last changes fastest.
Arguments:
- query: bfloat16 [36864, 2048], P(('dp', 'seq')), may hold values from -32 to 32
- key_in: bfloat16 [36864, 2048], P(('dp', 'seq')), may hold values from -6.5 to 6.5
- value: bfloat16 [36864, 2048], P(('dp', 'seq')), may hold values from -6 to 6
- out_weight: bfloat16 [2048, 3072], P('dp'), may hold values from -0.125 to 0.125
- out_grad: bfloat16 [36864, 3072], P(('dp', 'seq')), may hold values from -6 to 6
- windows: int32 [96, 5], P('dp'), may hold values from 0 to 95, as said below
- window_count: int32 [96], P('dp'), may hold values from 1 to 5, as said below
Outputs:
- output: bfloat16 [36864, 3072], P(('dp', 'seq'))
- d_query: bfloat16 [36864, 2048], P(('dp', 'seq'))
- d_key: bfloat16 [36864, 2048], P(('dp', 'seq'))
- d_value: bfloat16 [36864, 2048], P(('dp', 'seq'))
Inputs may be any that keep to these rules, and one draw needn't show every extreme that they name: `windows`: row t names 5 different tiles; its first entry is t itself, and every entry lies in tile t's slab or in the slab just before or after it, a slab being 3 consecutive tiles. Tile t attends to the first window_count[t] tiles of its row; some tile attends to all 5 and some to one.
All inputs are finite; a program needn't handle non-finite values.
Results may differ from a plain program's by a relative error of at most 0.0075.
Values may be sent and summed in bfloat16 or wider, within the bound.
A program may use at most 192 MiB of HBM per device.

v0:
```python
import jax
import jax.numpy as jnp
from jax import lax
from jax.sharding import PartitionSpec as P

HD = 128
TILE = 384


def extended_2(block, sides, width):
    for axis, dim in sides:
        count = lax.axis_size(axis)
        forward = [(i, i + 1) for i in range(count - 1)]
        backward = [(target, source) for source, target in forward]
        low = lax.ppermute(
            lax.slice_in_dim(block, block.shape[dim] - width, None, axis=dim), axis, forward
        )
        high = lax.ppermute(lax.slice_in_dim(block, 0, width, axis=dim), axis, backward)
        block = jnp.concatenate([low, block, high], axis=dim)
    return block


def make_fold(source, out_grad, portion):
    out_sum = jnp.dot(source, portion, preferred_element_type=jnp.float32)
    product = jnp.einsum("td,rd->tr", out_grad, portion, preferred_element_type=jnp.float32).astype(
        jnp.bfloat16
    )
    return (out_sum, product)


def body(query, key_in, value, out_weight, out_grad, windows, window_count):
    tile_count = windows.shape[0]
    window = windows.shape[1]
    factor = HD ** (-0.5)
    q_heads, k_heads, v_heads = (
        lax.all_to_all(query, "seq", split_axis=1, concat_axis=0, tiled=True),
        lax.all_to_all(key_in, "seq", split_axis=1, concat_axis=0, tiled=True),
        lax.all_to_all(value, "seq", split_axis=1, concat_axis=0, tiled=True),
    )
    slab_rows = q_heads.shape[0]
    width_local = q_heads.shape[1]
    head_count = width_local // HD
    stacked = jnp.concatenate([k_heads, v_heads], axis=1)
    extended = extended_2(stacked, (("dp", 0),), slab_rows)
    blocks = extended.reshape(3 * tile_count, TILE, 2, head_count, HD)
    lowest = (lax.axis_index("dp") - 1) * tile_count
    local_ids = windows - lowest
    query_tiles = q_heads.reshape(tile_count, TILE, head_count, HD)

    def forward_tile(members):
        query_tile, tile_ids, filled = members
        gathered = blocks[tile_ids]
        keyed_rows = gathered[:, :, 0]
        value_rows = gathered[:, :, 1]
        scores = (
            jnp.einsum("qhd,wkhd->hqwk", query_tile, keyed_rows, preferred_element_type=jnp.float32)
            * factor
        )
        allowed = (jnp.arange(window) < filled)[None, None, :, None]
        scores = jnp.where(allowed, scores, -jnp.inf)
        largest = jnp.max(scores, axis=(2, 3), keepdims=True)
        raised = jnp.exp(scores - largest)
        total = jnp.sum(raised, axis=(2, 3), keepdims=True)
        weights = raised / total
        attn_tile = jnp.einsum(
            "hqwk,wkhd->qhd",
            weights.astype(jnp.bfloat16),
            value_rows,
            preferred_element_type=jnp.float32,
        ).astype(jnp.bfloat16)
        return (attn_tile, weights, largest[:, :, 0, 0], total[:, :, 0, 0])

    attn_tiles, saved_weights, saved_largest, saved_total = lax.map(
        forward_tile, (query_tiles, local_ids, window_count)
    )
    attn_heads = attn_tiles.reshape(slab_rows, width_local)
    attn_tokens = lax.all_to_all(attn_heads, "seq", split_axis=0, concat_axis=1, tiled=True)
    out_sum, grad_tokens = make_fold(
        attn_tokens, out_grad, lax.all_gather(out_weight, "dp", axis=0, tiled=True)
    )
    output = out_sum.astype(jnp.bfloat16)
    grad_heads = lax.all_to_all(grad_tokens, "seq", split_axis=1, concat_axis=0, tiled=True)
    grad_tiles = grad_heads.reshape(tile_count, TILE, head_count, HD)

    def backward_tile(members):
        query_tile, tile_ids, weights, grad_tile = members
        gathered = blocks[tile_ids]
        keyed_rows = gathered[:, :, 0]
        value_rows = gathered[:, :, 1]
        rounded = weights.astype(jnp.bfloat16)
        grad_weights = jnp.einsum(
            "qhd,wkhd->hqwk", grad_tile, value_rows, preferred_element_type=jnp.float32
        )
        centre = jnp.sum(weights * grad_weights, axis=(2, 3), keepdims=True)
        grad_scores = (weights * (grad_weights - centre) * factor).astype(jnp.bfloat16)
        grad_query = jnp.einsum(
            "hqwk,wkhd->qhd", grad_scores, keyed_rows, preferred_element_type=jnp.float32
        ).astype(jnp.bfloat16)
        grad_keyed = jnp.einsum(
            "hqwk,qhd->wkhd", grad_scores, query_tile, preferred_element_type=jnp.float32
        )
        grad_valued = jnp.einsum(
            "hqwk,qhd->wkhd", rounded, grad_tile, preferred_element_type=jnp.float32
        )
        return (grad_query, grad_keyed, grad_valued, centre[:, :, 0, 0])

    query_grads, keyed_parts, valued_parts, saved_centre = lax.map(
        backward_tile, (query_tiles, local_ids, saved_weights, grad_tiles)
    )
    flat_size = TILE * width_local
    onehot = (local_ids.reshape(-1)[:, None] == jnp.arange(3 * tile_count)[None, :]).astype(
        jnp.float32
    )
    keyed_ext = jnp.einsum(
        "ns,nx->sx",
        onehot,
        keyed_parts.reshape(tile_count * window, flat_size),
        precision=lax.Precision.HIGHEST,
    ).reshape(3 * slab_rows, width_local)
    valued_ext = jnp.einsum(
        "ns,nx->sx",
        onehot,
        valued_parts.reshape(tile_count * window, flat_size),
        precision=lax.Precision.HIGHEST,
    ).reshape(3 * slab_rows, width_local)
    combined = jnp.concatenate([keyed_ext, valued_ext], axis=1)
    outer_rims = jnp.concatenate([combined[:slab_rows], combined[2 * slab_rows :]], axis=0)
    arrived = extended_2(outer_rims.astype(jnp.bfloat16), (("dp", 0),), slab_rows).astype(
        outer_rims.dtype
    )
    summed = combined[slab_rows : 2 * slab_rows] + arrived[:slab_rows] + arrived[3 * slab_rows :]
    key_heads = summed[:, :width_local].astype(jnp.bfloat16)
    value_heads = summed[:, width_local:].astype(jnp.bfloat16)
    query_heads = query_grads.reshape(slab_rows, width_local)
    d_query, d_key, d_value = (
        lax.all_to_all(query_heads, "seq", split_axis=0, concat_axis=1, tiled=True),
        lax.all_to_all(key_heads, "seq", split_axis=0, concat_axis=1, tiled=True),
        lax.all_to_all(value_heads, "seq", split_axis=0, concat_axis=1, tiled=True),
    )
    return (output, d_query, d_key, d_value)


def solution(mesh):
    in_specs = (
        P(("dp", "seq"), None),
        P(("dp", "seq"), None),
        P(("dp", "seq"), None),
        P("dp", None),
        P(("dp", "seq"), None),
        P("dp", None),
        P("dp"),
    )
    out_specs = (
        P(("dp", "seq"), None),
        P(("dp", "seq"), None),
        P(("dp", "seq"), None),
        P(("dp", "seq"), None),
    )
    return jax.shard_map(body, mesh=mesh, in_specs=in_specs, out_specs=out_specs, check_vma=False)
```

profile of v0, /device:TPU:32, one launch (start us, length us, event | category | flops | bytes accessed | tf_op | source)
XLA Modules:
  0.0 523.9 jit_solution(6442156912303026273)
XLA Ops:
  9.9 10.0 %all-to-all-start.1 = ((bf16[144,8,256]{2,0,1:T(8,128)(2,1)}), bf16[144,8,256]{2,0,1:T(8,128)(2,1)S(1)}, u32[]{:S(2)}, u32[]{:S(2)}) async-start(bf16[144,8,256]{2,0,1:T(8,128)(2,1)} %bitcast.149), calls=%async_computation.1 | async-start | bytes 1179648 | tf_op jit(solution)/shard_map/all_to_all | solution.py:38
  21.0 24.1 %all-to-all-done.1 = bf16[144,8,256]{2,0,1:T(8,128)(2,1)S(1)} async-done(((bf16[144,8,256]{2,0,1:T(8,128)(2,1)}), bf16[144,8,256]{2,0,1:T(8,128)(2,1)S(1)}, u32[]{:S(2)}, u32[]{:S(2)}) %all-to-all-start.1) | async-done | bytes 589856 | tf_op jit(solution)/shard_map/all_to_all | solution.py:38
  45.1 28.5 %all_to_all.146 = bf16[144,8,256]{2,0,1:T(8,128)(2,1)S(1)} all-to-all(bf16[144,8,256]{2,0,1:T(8,128)(2,1)S(1)} %bitcast.210), channel_id=1, replica_groups=mesh['dp'=32,'seq'=8] {'seq'}, dimensions={1} | all-to-all | bytes 1179648 | tf_op jit(solution)/shard_map/all_to_all | solution.py:37
  84.1 64.2 %all-to-all-done.2 = bf16[144,8,256]{2,0,1:T(8,128)(2,1)S(1)} async-done(((bf16[144,8,256]{2,0,1:T(8,128)(2,1)}), bf16[144,8,256]{2,0,1:T(8,128)(2,1)S(1)}, u32[]{:S(2)}, u32[]{:S(2)}) %all-to-all-start.2) | async-done | bytes 589856 | tf_op jit(solution)/shard_map/all_to_all | solution.py:36
  152.0 8.4 %reshape.123 = bf16[9,384,2,2,128]{4,3,2,1,0:T(2,128)(2,1)} reshape(bf16[3456,512]{1,0:T(8,128)(2,1)} %pad_maximum_fusion) | data formatting | bytes 7077888 | tf_op jit(solution)/shard_map/reshape | solution.py:45
  164.9 8.9 %convolution_convert_fusion.1 = bf16[144,2048]{1,0:T(8,128)(2,1)S(1)} fusion(bf16[144,3072]{1,0:T(8,128)(2,1)S(1)} %copy-done, bf16[2048,3072]{1,0:T(8,128)(2,1)} %all-gather.2.cloned.1.call-done), kind=kOutput, calls=%fused_computation.55 | convolution fusion | flops 1812234240 | bytes 14057472 | tf_op jit(solution)/shard_map/td,rd->tr/dot_general | solution.py:25
  174.7 7.7 %all-to-all-start.4 = ((bf16[144,8,256]{2,0,1:T(8,128)(2,1)}), bf16[144,8,256]{2,0,1:T(8,128)(2,1)}, u32[]{:S(2)}, u32[]{:S(2)}) async-start(bf16[144,8,256]{2,0,1:T(8,128)(2,1)} %bitcast.147), calls=%async_computation.4 | async-start | bytes 1179648 | tf_op jit(solution)/shard_map/all_to_all | solution.py:82
  183.5 64.0 %while.26 = (s32[]{:T(128)}, bf16[3,384,2,128]{3,2,1,0:T(2,128)(2,1)}, f32[3,2,384,5,384]{2,4,3,1,0:T(8,128)}, s32[3,5]{1,0:T(4,128)S(1)}, bf16[9,384,2,2,128]{4...) while((s32[]{:T(128)}, bf16[3,384,2,128]{3,2,1,0:T(2,128)(2,1)}, ...), condition=%wide.region_3.4_spmd, body=%wide.region_0.3_spmd.sunk | while | flops 778665472 | bytes 66479360 | solution.py:73
  198.4 6.5 %bitcast_dynamic-update-slice_fusion.2 = f32[3,2,384,5,384]{2,4,3,1,0:T(8,128)} fusion(f32[3,2,384,5,384]{2,4,3,1,0:T(8,128)} %get-tuple-element.357, s32[]{:T(128)S(6)} %copy.236, f32[2,384]{1,0:T(2,128)S(1)} %fusion.72, f32[2,384]{1,0:T(2,128)S(1)} %get-tuple-element.331, f32[2,384,5,384]{1,3,2,0:T(8,128)} %copy-done.2, ...), kind=kLoop, calls=%fused_computation.2.clone.1 | loop fusion | flops 5898240 | bytes 11802633 | tf_op jit(solution)/shard_map/while/body/jit(dynamic_update_index_in_dim)/dynamic_update_slice | solution.py:73
  219.8 6.4 %bitcast_dynamic-update-slice_fusion.2 = f32[3,2,384,5,384]{2,4,3,1,0:T(8,128)} fusion(f32[3,2,384,5,384]{2,4,3,1,0:T(8,128)} %get-tuple-element.357, s32[]{:T(128)S(6)} %copy.236, f32[2,384]{1,0:T(2,128)S(1)} %fusion.72, f32[2,384]{1,0:T(2,128)S(1)} %get-tuple-element.331, f32[2,384,5,384]{1,3,2,0:T(8,128)} %copy-done.2, ...), kind=kLoop, calls=%fused_computation.2.clone.1 | loop fusion | flops 5898240 | bytes 11802633 | tf_op jit(solution)/shard_map/while/body/jit(dynamic_update_index_in_dim)/dynamic_update_slice | solution.py:73
  241.1 6.4 %bitcast_dynamic-update-slice_fusion.2 = f32[3,2,384,5,384]{2,4,3,1,0:T(8,128)} fusion(f32[3,2,384,5,384]{2,4,3,1,0:T(8,128)} %get-tuple-element.357, s32[]{:T(128)S(6)} %copy.236, f32[2,384]{1,0:T(2,128)S(1)} %fusion.72, f32[2,384]{1,0:T(2,128)S(1)} %get-tuple-element.331, f32[2,384,5,384]{1,3,2,0:T(8,128)} %copy-done.2, ...), kind=kLoop, calls=%fused_computation.2.clone.1 | loop fusion | flops 5898240 | bytes 11802633 | tf_op jit(solution)/shard_map/while/body/jit(dynamic_update_index_in_dim)/dynamic_update_slice | solution.py:73
  250.4 104.2 %while.27 = (s32[]{:T(128)}, bf16[3,384,2,128]{3,2,1,0:T(2,128)(2,1)}, f32[3,5,384,2,128]{4,3,2,1,0:T(2,128)}, f32[3,5,384,2,128]{4,3,2,1,0:T(2,128)}, s32[3,5]{...) while((s32[]{:T(128)}, ...), condition=%wide.region_6.7_spmd, body=%wide.region_4.6_spmd.sunk | while | flops 1518895360 | bytes 78260528 | solution.py:107
  258.7 5.4 %fusion.81 = bf16[2,384,5,384]{1,3,2,0:T(8,128)(2,1)} fusion(f32[2,384,5,384]{1,3,2,0:T(8,128)S(1)} %get-tuple-element.342, f32[3,2,384,5,384]{2,4,3,1,0:T(8,128)} %get-tuple-element.397, s32[]{:T(128)S(6)} %copy.246, f32[2,384]{1,0:T(2,128)S(1)} %get-tuple-element.343), kind=kLoop, calls=%fused_computation.30.clone.1 | loop fusion | flops 5898240 | bytes 14748676 | tf_op jit(solution)/shard_map/while/body/eval_jaxpr/convert_element_type | solution.py:95
  293.4 5.4 %fusion.81 = bf16[2,384,5,384]{1,3,2,0:T(8,128)(2,1)} fusion(f32[2,384,5,384]{1,3,2,0:T(8,128)S(1)} %get-tuple-element.342, f32[3,2,384,5,384]{2,4,3,1,0:T(8,128)} %get-tuple-element.397, s32[]{:T(128)S(6)} %copy.246, f32[2,384]{1,0:T(2,128)S(1)} %get-tuple-element.343), kind=kLoop, calls=%fused_computation.30.clone.1 | loop fusion | flops 5898240 | bytes 14748676 | tf_op jit(solution)/shard_map/while/body/eval_jaxpr/convert_element_type | solution.py:95
  354.7 8.6 %reshape.126 = f32[15,98304]{1,0:T(8,128)} reshape(f32[3,5,384,2,128]{4,3,2,1,0:T(2,128)} %get-tuple-element.94) | data formatting | bytes 11796480 | tf_op jit(solution)/shard_map/reshape | solution.py:117
  363.2 8.1 %fusion.35 = f32[9,98304]{1,0:T(8,128)} fusion(f32[15,98304]{1,0:T(8,128)} %reshape.126, s32[15]{0:T(128)S(1)} %copy-done.8), kind=kOutput, calls=%fused_computation.69 | convolution fusion | flops 159252608 | bytes 9437244 | tf_op jit(solution)/shard_map/ns,nx->sx/dot_general | solution.py:114
  379.9 8.5 %reshape.128 = f32[15,98304]{1,0:T(8,128)} reshape(f32[3,5,384,2,128]{4,3,2,1,0:T(2,128)} %get-tuple-element.95) | data formatting | bytes 11796480 | tf_op jit(solution)/shard_map/reshape | solution.py:123
  388.4 8.1 %fusion.34 = f32[9,98304]{1,0:T(8,128)} fusion(f32[15,98304]{1,0:T(8,128)} %reshape.128, s32[15]{0:T(128)S(1)} %copy-done.8), kind=kOutput, calls=%fused_computation.68 | convolution fusion | flops 159252608 | bytes 9437244 | tf_op jit(solution)/shard_map/ns,nx->sx/dot_general | solution.py:120
  413.9 9.6 %all-to-all-start.3 = ((bf16[8,144,256]{2,1,0:T(8,128)(2,1)}), bf16[8,144,256]{2,1,0:T(8,128)(2,1)S(1)}, u32[]{:S(2)}, u32[]{:S(2)}) async-start(bf16[8,144,256]{2,1,0:T(8,128)(2,1)} %all_to_all.119), calls=%async_computation.3 | async-start | bytes 1179648 | tf_op jit(solution)/shard_map/all_to_all | solution.py:77
  426.3 32.6 %all-to-all-done.3 = bf16[8,144,256]{2,1,0:T(8,128)(2,1)S(1)} async-done(((bf16[8,144,256]{2,1,0:T(8,128)(2,1)}), bf16[8,144,256]{2,1,0:T(8,128)(2,1)S(1)}, u32[]{:S(2)}, u32[]{:S(2)}) %all-to-all-start.3) | async-done | bytes 589856 | tf_op jit(solution)/shard_map/all_to_all | solution.py:77
  463.2 6.8 %fusion.33 = bf16[1152,512]{1,0:T(8,128)(2,1)S(1)} fusion(f32[3456,512]{1,0:T(8,128)} %constant_dynamic-update-slice_fusion.4, bf16[1152,512]{1,0:T(8,128)(2,1)} %collective-permute-done.3, bf16[1152,512]{1,0:T(8,128)(2,1)S(1)} %get-tuple-element.225, bf16[1152,512]{1,0:T(8,128)(2,1)S(1)} %get-tuple-element.226, bf16[1152,512]{1,0:T(8,128)(2,1)} %collective-permute-done.2), kind=kLoop, calls=%fused_computation.58 | loop fusion | flops 11206656 | bytes 8257536 | tf_op jit(solution)/shard_map/convert.1
  470.8 8.0 %all-to-all-done.5 = bf16[8,144,256]{2,1,0:T(8,128)(2,1)} async-done(((bf16[8,144,256]{2,1,0:T(8,128)(2,1)}), bf16[8,144,256]{2,1,0:T(8,128)(2,1)}, u32[]{:S(2)}, u32[]{:S(2)}) %all-to-all-start.5) | async-done | bytes 589856 | tf_op jit(solution)/shard_map/all_to_all | solution.py:136
  478.8 20.9 %all_to_all.147 = bf16[8,144,256]{2,1,0:T(8,128)(2,1)S(1)} all-to-all(bf16[8,144,256]{2,1,0:T(8,128)(2,1)S(1)} %bitcast.211), channel_id=1, replica_groups=mesh['dp'=32,'seq'=8] {'seq'}, dimensions={0} | all-to-all | bytes 1179648 | tf_op jit(solution)/shard_map/all_to_all | solution.py:137
  503.4 7.6 %convolution_convert_fusion = bf16[144,3072]{1,0:T(8,128)(2,1)} fusion(bf16[144,2048]{1,0:T(8,128)(2,1)S(1)} %bitcast.205, bf16[2048,3072]{1,0:T(8,128)(2,1)} %all-gather.2.cloned.1.call-done), kind=kOutput, calls=%fused_computation.53 | convolution fusion | flops 1812381696 | bytes 14057472 | tf_op jit(solution)/shard_map/dot_general | solution.py:24
  (174 shorter events, 207.7 us)
Async XLA Ops:
  7.2 157.8 %copy-start = (bf16[144,3072]{1,0:T(8,128)(2,1)S(1)}, bf16[144,3072]{1,0:T(8,128)(2,1)}, u32[]{:S(2)}) copy-start(bf16[144,3072]{1,0:T(8,128)(2,1)} %param.15) | copy-start | bytes 2654212
  7.2 71.8 %copy-start.7 = (bf16[144,2048]{1,0:T(8,128)(2,1)S(1)}, bf16[144,2048]{1,0:T(8,128)(2,1)}, u32[]{:S(2)}) copy-start(bf16[144,2048]{1,0:T(8,128)(2,1)} %param.11) | copy-start | bytes 1769476
  7.2 76.3 %copy-start.9 = (s32[3,5]{1,0:T(4,128)S(1)}, s32[3,5]{1,0:T(4,128)}, u32[]{:S(2)}) copy-start(s32[3,5]{1,0:T(4,128)} %param.16) | copy-start | bytes 184
  7.2 157.7 %all-gather.2.cloned.1.call-start = ((), (), s32[]{:S(2)}) async-start(), calls=%async_computation.8 | async-start | bytes 12976128 | tf_op jit(solution)/shard_map/all_gather | solution.py:79
  9.9 35.2 %all-to-all-start.1 = ((bf16[144,8,256]{2,0,1:T(8,128)(2,1)}), bf16[144,8,256]{2,0,1:T(8,128)(2,1)S(1)}, u32[]{:S(2)}, u32[]{:S(2)}) async-start(bf16[144,8,256]{2,0,1:T(8,128)(2,1)} %bitcast.149), calls=%async_computation.1 | async-start | bytes 1179648 | tf_op jit(solution)/shard_map/all_to_all | solution.py:38
  74.7 73.8 %collective-permute-start.1 = (bf16[1152,512]{1,0:T(8,128)(2,1)}, bf16[1152,512]{1,0:T(8,128)(2,1)}, u32[]{:S(2)}, u32[]{:S(2)}) collective-permute-start(bf16[1152,512]{1,0:T(8,128)(2,1)} %pad_maximum_fusion.4), channel_id=1, source_target_pairs={{8,0},{16,8},{24,16},{32,24},{40,32},{48,40},{56,48},{64,56},{72,6... | collective-permute-start | bytes 3538952 | tf_op jit(solution)/shard_map/ppermute | solution.py:18
  76.6 71.9 %collective-permute-start = (bf16[1152,512]{1,0:T(8,128)(2,1)}, bf16[1152,512]{1,0:T(8,128)(2,1)}, u32[]{:S(2)}, u32[]{:S(2)}) collective-permute-start(bf16[1152,512]{1,0:T(8,128)(2,1)} %pad_maximum_fusion.4), channel_id=1, source_target_pairs={{0,8},{8,16},{16,24},{24,32},{32,40},{40,48},{48,56},{56,64},{64,7... | collective-permute-start | bytes 3538952 | tf_op jit(solution)/shard_map/ppermute | solution.py:15
  79.9 68.4 %all-to-all-start.2 = ((bf16[144,8,256]{2,0,1:T(8,128)(2,1)}), bf16[144,8,256]{2,0,1:T(8,128)(2,1)S(1)}, u32[]{:S(2)}, u32[]{:S(2)}) async-start(bf16[144,8,256]{2,0,1:T(8,128)(2,1)} %bitcast.148), calls=%async_computation.2 | async-start | bytes 1179648 | tf_op jit(solution)/shard_map/all_to_all | solution.py:36
  164.9 18.6 %copy-start.10 = (s32[3]{0:T(128)S(1)}, s32[3]{0:T(128)}, u32[]{:S(2)}) copy-start(s32[3]{0:T(128)} %param.17) | copy-start | bytes 40
  174.7 72.9 %all-to-all-start.4 = ((bf16[144,8,256]{2,0,1:T(8,128)(2,1)}), bf16[144,8,256]{2,0,1:T(8,128)(2,1)}, u32[]{:S(2)}, u32[]{:S(2)}) async-start(bf16[144,8,256]{2,0,1:T(8,128)(2,1)} %bitcast.147), calls=%async_computation.4 | async-start | bytes 1179648 | tf_op jit(solution)/shard_map/all_to_all | solution.py:82
  250.6 8.1 %copy-start.4 = (bf16[3,384,2,128]{3,2,1,0:T(2,128)(2,1)}, bf16[3,384,2,128]{3,2,1,0:T(2,128)(2,1)S(1)}, u32[]{:S(2)}) copy-start(bf16[3,384,2,128]{3,2,1,0:T(2,128)(2,1)S(1)} %get-tuple-element.398) | copy-start | bytes 1769476 | tf_op jit(solution)/shard_map/while
  278.1 7.2 %copy-start.5 = (bf16[3,384,2,128]{3,2,1,0:T(2,128)(2,1)S(1)}, bf16[3,384,2,128]{3,2,1,0:T(2,128)(2,1)}, u32[]{:S(2)}) copy-start(bf16[3,384,2,128]{3,2,1,0:T(2,128)(2,1)} %copy-done.4) | copy-start | bytes 1769476 | tf_op jit(solution)/shard_map/while
  285.3 8.1 %copy-start.4 = (bf16[3,384,2,128]{3,2,1,0:T(2,128)(2,1)}, bf16[3,384,2,128]{3,2,1,0:T(2,128)(2,1)S(1)}, u32[]{:S(2)}) copy-start(bf16[3,384,2,128]{3,2,1,0:T(2,128)(2,1)S(1)} %get-tuple-element.398) | copy-start | bytes 1769476 | tf_op jit(solution)/shard_map/while
  312.7 7.3 %copy-start.5 = (bf16[3,384,2,128]{3,2,1,0:T(2,128)(2,1)S(1)}, bf16[3,384,2,128]{3,2,1,0:T(2,128)(2,1)}, u32[]{:S(2)}) copy-start(bf16[3,384,2,128]{3,2,1,0:T(2,128)(2,1)} %copy-done.4) | copy-start | bytes 1769476 | tf_op jit(solution)/shard_map/while
  320.0 8.1 %copy-start.4 = (bf16[3,384,2,128]{3,2,1,0:T(2,128)(2,1)}, bf16[3,384,2,128]{3,2,1,0:T(2,128)(2,1)S(1)}, u32[]{:S(2)}) copy-start(bf16[3,384,2,128]{3,2,1,0:T(2,128)(2,1)S(1)} %get-tuple-element.398) | copy-start | bytes 1769476 | tf_op jit(solution)/shard_map/while
  347.4 7.3 %copy-start.5 = (bf16[3,384,2,128]{3,2,1,0:T(2,128)(2,1)S(1)}, bf16[3,384,2,128]{3,2,1,0:T(2,128)(2,1)}, u32[]{:S(2)}) copy-start(bf16[3,384,2,128]{3,2,1,0:T(2,128)(2,1)} %copy-done.4) | copy-start | bytes 1769476 | tf_op jit(solution)/shard_map/while
  354.7 8.6 %copy-start.8 = (s32[15]{0:T(128)S(1)}, s32[15]{0:T(128)}, u32[]{:S(2)}) copy-start(s32[15]{0:T(128)} %eq.15) | copy-start | bytes 184
  404.7 8.0 %copy-start.6 = (bf16[3,384,2,128]{3,2,1,0:T(2,128)(2,1)S(1)}, bf16[3,384,2,128]{3,2,1,0:T(2,128)(2,1)}, u32[]{:S(2)}) copy-start(bf16[3,384,2,128]{3,2,1,0:T(2,128)(2,1)} %get-tuple-element.91) | copy-start | bytes 1769476
  408.4 54.8 %collective-permute-start.3 = (bf16[1152,512]{1,0:T(8,128)(2,1)S(1)}, bf16[1152,512]{1,0:T(8,128)(2,1)}, u32[]{:S(2)}, u32[]{:S(2)}) collective-permute-start(bf16[1152,512]{1,0:T(8,128)(2,1)S(1)} %get-tuple-element.226), channel_id=1, source_target_pairs={{8,0},{16,8},{24,16},{32,24},{40,32},{48,40},{56,48},{64,56},{72,6... | collective-permute-start | bytes 3538952 | tf_op jit(solution)/shard_map/ppermute | solution.py:18
  410.3 52.8 %collective-permute-start.2 = (bf16[1152,512]{1,0:T(8,128)(2,1)S(1)}, bf16[1152,512]{1,0:T(8,128)(2,1)}, u32[]{:S(2)}, u32[]{:S(2)}) collective-permute-start(bf16[1152,512]{1,0:T(8,128)(2,1)S(1)} %get-tuple-element.225), channel_id=1, source_target_pairs={{0,8},{8,16},{16,24},{24,32},{32,40},{40,48},{48,56},{56,64},{64,7... | collective-permute-start | bytes 3538952 | tf_op jit(solution)/shard_map/ppermute | solution.py:15
  413.9 45.0 %all-to-all-start.3 = ((bf16[8,144,256]{2,1,0:T(8,128)(2,1)}), bf16[8,144,256]{2,1,0:T(8,128)(2,1)S(1)}, u32[]{:S(2)}, u32[]{:S(2)}) async-start(bf16[8,144,256]{2,1,0:T(8,128)(2,1)} %all_to_all.119), calls=%async_computation.3 | async-start | bytes 1179648 | tf_op jit(solution)/shard_map/all_to_all | solution.py:77
  458.9 19.9 %all-to-all-start.5 = ((bf16[8,144,256]{2,1,0:T(8,128)(2,1)}), bf16[8,144,256]{2,1,0:T(8,128)(2,1)}, u32[]{:S(2)}, u32[]{:S(2)}) async-start(bf16[8,144,256]{2,1,0:T(8,128)(2,1)} %all_to_all.126), calls=%async_computation.5 | async-start | bytes 1179648 | tf_op jit(solution)/shard_map/all_to_all | solution.py:136
  499.8 15.9 %all-to-all-start.7 = ((bf16[8,144,256]{2,1,0:T(8,128)(2,1)}), bf16[8,144,256]{2,1,0:T(8,128)(2,1)S(1)}, u32[]{:S(2)}, u32[]{:S(2)}) async-start(bf16[8,144,256]{2,1,0:T(8,128)(2,1)} %bitcast.43), calls=%async_computation.7 | async-start | bytes 1179648 | tf_op jit(solution)/shard_map/all_to_all | solution.py:138
  503.4 13.2 %copy-start.1 = (bf16[144,3072]{1,0:T(8,128)(2,1)S(1)}, bf16[144,3072]{1,0:T(8,128)(2,1)}, u32[]{:S(2)}) copy-start(bf16[144,3072]{1,0:T(8,128)(2,1)} %param.15) | copy-start | bytes 2654212
  (6 other events, 23.7 us)
Sparse Core Ops, SparseCore 0:
  9.9 140.2 all-gather.1
where the time goes:
time: 531 us; the launch traced here: 524 us
  local copies, waits for them, and re-layouts  141 us (27%)
  waiting for transfers between devices  132 us (25%)
  matrix products  82.6 us (16%)
  other arithmetic  56.4 us (11%)
  blocking collectives  49.4 us (9%)
  starting transfers between devices  47.3 us (9%)
  between operations  14.7 us (3%)
    all_to_all x1, waiting for transfers between devices, body(): lax.all_to_all(query, 'seq', split_axis=1, concat_axis=0, tiled=True)  64.2 us
    all_to_all x1, waiting for transfers between devices, body(): lax.all_to_all(attn_heads, 'seq', split_axis=0, concat_axis=1, tiled=True)  32.6 us
    dynamic_update_slice x9, local copies, waits for them, and re-layouts, body(): lax.map(backward_tile, (query_tiles, local_ids, saved_weights, grad_tiles))  30.4 us
    all_to_all x1, blocking collectives, body(): lax.all_to_all(key_in, 'seq', split_axis=1, concat_axis=0, tiled=True)  28.5 us
    all_to_all x1, waiting for transfers between devices, body(): lax.all_to_all(value, 'seq', split_axis=1, concat_axis=0, tiled=True)  24.1 us
    all_to_all x1, blocking collectives, body(): lax.all_to_all(key_heads, 'seq', split_axis=0, concat_axis=1, tiled=True)  20.9 us
    dynamic_update_slice x3, other arithmetic, body(): lax.map(forward_tile, (query_tiles, local_ids, window_count))  19.3 us
    convert_element_type x3, other arithmetic, backward_tile(): (weights * (grad_weights - centre) * factor).astype(jnp.bfloat16)  16.2 us
  transfers between devices with their start and end apart: 11, of which 5 were waited for; matrix products, arithmetic and copies ran while one was open for 19% of the time, Pallas kernels for 0%

commit v1 on v0

v1 whole, which is shorter than its diff:
```python
import jax, jax.numpy as jnp
from jax import lax
from jax.experimental import pallas as pl
from jax.experimental.pallas import tpu as pltpu
from jax.sharding import PartitionSpec as P
HD=128; TILE=384; WIN=5
LOG2E=1.4426950408889634
def dotT(a,b): return lax.dot_general(a,b,(((1,),(1,)),((),())),preferred_element_type=jnp.float32)
def dot0(a,b): return lax.dot_general(a,b,(((0,),(0,)),((),())),preferred_element_type=jnp.float32)
def dot(a,b): return jnp.dot(a,b,preferred_element_type=jnp.float32)

def attend(ids, counts, q_ref, g_ref, k_ref, v_ref, attn_ref, dq_ref, dk_ref, dv_ref, s_buf, e_buf):
    factor = HD ** -0.5
    t = pl.program_id(1)
    @pl.when(t == 0)
    def _():
        dk_ref[...] = jnp.zeros_like(dk_ref)
        dv_ref[...] = jnp.zeros_like(dv_ref)
    q = q_ref[...]; g = g_ref[...]
    count = counts[t]
    top = None
    for j in range(WIN):
        rows = pl.ds(pl.multiple_of(ids[t, j] * TILE, TILE), TILE)
        s = dotT(q, k_ref[rows, :])
        if j > 0:
            s = s + jnp.where(j < count, 0.0, -jnp.inf).astype(jnp.float32)
        s_buf[j] = s
        m = jnp.max(s, axis=1, keepdims=True)
        top = m if top is None else jnp.maximum(top, m)
    total = jnp.zeros((TILE, 1), jnp.float32)
    acc = jnp.zeros((TILE, HD), jnp.float32)
    for j in range(WIN):
        rows = pl.ds(pl.multiple_of(ids[t, j] * TILE, TILE), TILE)
        e = jnp.exp2((s_buf[j] - top) * (factor * LOG2E))
        total = total + jnp.sum(e, axis=1, keepdims=True)
        eb = e.astype(jnp.bfloat16)
        e_buf[j] = eb
        acc = acc + dot(eb, v_ref[rows, :])
    inv = 1.0 / total
    attn = acc * inv
    attn_ref[...] = attn.astype(jnp.bfloat16)
    gf = g.astype(jnp.float32)
    centre = jnp.sum(gf * attn, axis=1, keepdims=True)
    gs = (gf * inv).astype(jnp.bfloat16)
    qs = (q.astype(jnp.float32) * (inv * factor)).astype(jnp.bfloat16)
    dq = jnp.zeros((TILE, HD), jnp.float32)
    for j in range(WIN):
        rows = pl.ds(pl.multiple_of(ids[t, j] * TILE, TILE), TILE)
        dp = dotT(g, v_ref[rows, :])
        eb = e_buf[j]
        ds = (eb.astype(jnp.float32) * (dp - centre)).astype(jnp.bfloat16)
        dq = dq + dot(ds, k_ref[rows, :])
        dk_ref[rows, :] += dot0(ds, qs)
        dv_ref[rows, :] += dot0(eb, gs)
    dq_ref[...] = (dq * (inv * factor)).astype(jnp.bfloat16)

def attention(q, g, k, v, ids, counts):
    rows, width = q.shape
    ext = k.shape[0]
    heads = width // HD; tiles = rows // TILE
    qs = pl.BlockSpec((TILE, HD), lambda h, t, *_: (t, h))
    ks = pl.BlockSpec((ext, HD), lambda h, t, *_: (0, h))
    bf = jax.ShapeDtypeStruct((rows, width), jnp.bfloat16)
    f32 = jax.ShapeDtypeStruct((ext, width), jnp.float32)
    return pl.pallas_call(
        attend,
        grid_spec=pltpu.PrefetchScalarGridSpec(
            num_scalar_prefetch=2, grid=(heads, tiles),
            in_specs=[qs, qs, ks, ks], out_specs=[qs, qs, ks, ks],
            scratch_shapes=[pltpu.VMEM((WIN, TILE, TILE), jnp.float32), pltpu.VMEM((WIN, TILE, TILE), jnp.bfloat16)]),
        out_shape=[bf, bf, f32, f32],
        compiler_params=pltpu.CompilerParams(vmem_limit_bytes=60 << 20),
        cost_estimate=pl.CostEstimate(flops=7_000_000_000*6, bytes_accessed=14_000_000, transcendentals=4_400_000),
    )(ids, counts, q, g, k, v)


def to_heads(x):
    return lax.all_to_all(x, "seq", split_axis=1, concat_axis=0, tiled=True)


def to_tokens(x):
    return lax.all_to_all(x, "seq", split_axis=0, concat_axis=1, tiled=True)


def with_neighbours(block, low_part, high_part):
    count = lax.axis_size("dp")
    up = [(i, i + 1) for i in range(count - 1)]
    down = [(b, a) for a, b in up]
    return lax.ppermute(low_part, "dp", up), lax.ppermute(high_part, "dp", down)


def body(query, key_in, value, out_weight, out_grad, windows, window_count):
    tiles = windows.shape[0]
    weight = lax.all_gather(out_weight, "dp", axis=0, tiled=True)
    k = to_heads(key_in)
    v = to_heads(value)
    kv = jnp.concatenate([k, v], axis=1)
    low, high = with_neighbours(kv, kv, kv)
    ext = jnp.concatenate([low, kv, high], axis=0)
    width = k.shape[1]
    rows = k.shape[0]
    q = to_heads(query)
    grad_tokens = lax.dot_general(out_grad, weight, (((1,), (1,)), ((), ())),
                                  preferred_element_type=jnp.float32).astype(jnp.bfloat16)
    g = to_heads(grad_tokens)
    ids = windows - (lax.axis_index("dp") - 1) * tiles
    attn, dq, dk, dv = attention(q, g, ext[:, :width], ext[:, width:], ids, window_count)
    attn_tokens = to_tokens(attn)
    d_kv = jnp.concatenate([dk, dv], axis=1)
    rim = d_kv.astype(jnp.bfloat16)
    low, high = with_neighbours(None, rim[2 * rows:], rim[:rows])
    output = jnp.dot(attn_tokens, weight, preferred_element_type=jnp.float32).astype(jnp.bfloat16)
    d_query = to_tokens(dq)
    summed = (d_kv[rows:2 * rows] + low.astype(jnp.float32) + high.astype(jnp.float32)).astype(jnp.bfloat16)
    return output, d_query, to_tokens(summed[:, :width]), to_tokens(summed[:, width:])


def solution(mesh):
    both = P(("dp", "seq"), None)
    return jax.shard_map(
        body, mesh=mesh, check_vma=False,
        in_specs=(both, both, both, P("dp", None), both, P("dp", None), P("dp")),
        out_specs=(both, both, both, both),
    )
```

time: 531 us -> 343 us (0.65); the launches traced: 524 us -> 342 us
  local copies, waits for them, and re-layouts: 141 us -> 21.8 us
  matrix products: 82.6 us -> 16.4 us
  other arithmetic: 56.4 us -> 7.97 us
  blocking collectives: 49.4 us -> 89.1 us
  Pallas kernels: 0 us -> 25.2 us
  waiting for transfers between devices: 132 us -> 121 us
    all_to_all x6 -> x5, waiting for transfers between devices: 131 us -> 59.7 us  [the longest x3 40.7 us: to_heads(): return lax.all_to_all(x, 'seq', split_axis=1, concat_axis=0, tiled=True)]
    dot_general x22 -> x2, matrix products: 82.6 us -> 16.4 us  [the longest x1 8.86 us: body(): lax.dot_general(out_grad, weight, (((1,), (1,)), ((), ())), preferred_ele...]
    ppermute x4, waiting for transfers between devices: 0.01 us -> 46.2 us  [the longest x2 46.2 us: with_neighbours(): lax.ppermute(high_part, 'dp', down)]
    all_to_all x2 -> x3, blocking collectives: 49.4 us -> 89.1 us  [the longest x2 60.7 us: to_tokens(): return lax.all_to_all(x, 'seq', split_axis=0, concat_axis=1, tiled=True)]
    dynamic_update_slice x21 -> x0, local copies, waits for them, and re-layouts: 36.3 us -> none  [the longest x9 30.4 us: body(): lax.map(backward_tile, (query_tiles, local_ids, saved_weights, grad_tiles))]
    reshape x7 -> x0, local copies, waits for them, and re-layouts: 35.8 us -> none  [the longest x1 8.57 us: body(): keyed_parts.reshape(tile_count * window, flat_size)]
    pallas_call x0 -> x1, Pallas kernels: none -> 25.2 us  [attention(): pl.pallas_call(attend, grid_spec=pltpu.PrefetchScalarGridSpec(num_scalar_...]
    dynamic_update_slice x3 -> x0, other arithmetic: 19.3 us -> none  [body(): lax.map(forward_tile, (query_tiles, local_ids, window_count))]
  transfers between devices with their start and end apart: 11 -> 10, of which waited for: 5 -> 6; matrix products, arithmetic and copies ran while one was open for 19% -> 11% of each run, Pallas kernels for 0% -> 0%
where the time goes in v1:
time: 343 us; the launch traced here: 342 us
  waiting for transfers between devices  121 us (35%)
  blocking collectives  89.1 us (26%)
  starting transfers between devices  45.9 us (13%)
  Pallas kernels  25.2 us (7%)
  local copies, waits for them, and re-layouts  21.8 us (6%)
  matrix products  16.4 us (5%)
  between operations  14.2 us (4%)
  other arithmetic  7.97 us (2%)
    all_to_all x2, blocking collectives, to_tokens(): return lax.all_to_all(x, 'seq', split_axis=0, concat_axis=1, tiled=True)  60.7 us
    ppermute x2, waiting for transfers between devices, with_neighbours(): lax.ppermute(high_part, 'dp', down)  46.2 us
    all_to_all x3, waiting for transfers between devices, to_heads(): return lax.all_to_all(x, 'seq', split_axis=1, concat_axis=0, tiled=True)  40.7 us
    all_to_all x1, blocking collectives, to_heads(): return lax.all_to_all(x, 'seq', split_axis=1, concat_axis=0, tiled=True)  28.5 us
    pallas_call x1, Pallas kernels, attention(): pl.pallas_call(attend, grid_spec=pltpu.PrefetchScalarGridSpec(num_scalar_...  25.2 us
    all_to_all x3, starting transfers between devices, to_heads(): return lax.all_to_all(x, 'seq', split_axis=1, concat_axis=0, tiled=True)  22.6 us
    all_to_all x2, waiting for transfers between devices, to_tokens(): return lax.all_to_all(x, 'seq', split_axis=0, concat_axis=1, tiled=True)  19 us
    all_gather x1, waiting for transfers between devices, body(): weight = lax.all_gather(out_weight, 'dp', axis=0, tiled=True)  14.9 us
  transfers between devices with their start and end apart: 10, of which 6 were waited for; matrix products, arithmetic and copies ran while one was open for 11% of the time, Pallas kernels for 0%

profile of v1, /device:TPU:32, one launch (start us, length us, event | category | flops | bytes accessed | tf_op | source)
XLA Modules:
  0.0 342.0 jit_solution(1750150202869911239)
XLA Ops:
  9.8 10.0 %all-to-all-start.2 = ((bf16[144,8,256]{2,0,1:T(8,128)(2,1)}), bf16[144,8,256]{2,0,1:T(8,128)(2,1)S(1)}, u32[]{:S(2)}, u32[]{:S(2)}) async-start(bf16[144,8,256]{2,0,1:T(8,128)(2,1)} %bitcast.45), calls=%async_computation.2 | async-start | bytes 1179648 | tf_op jit(solution)/shard_map/all_to_all | solution.py:78
  21.0 24.1 %all-to-all-done.2 = bf16[144,8,256]{2,0,1:T(8,128)(2,1)S(1)} async-done(((bf16[144,8,256]{2,0,1:T(8,128)(2,1)}), bf16[144,8,256]{2,0,1:T(8,128)(2,1)S(1)}, u32[]{:S(2)}, u32[]{:S(2)}) %all-to-all-start.2) | async-done | bytes 589856 | tf_op jit(solution)/shard_map/all_to_all | solution.py:78
  45.1 28.5 %all_to_all.152 = bf16[144,8,256]{2,0,1:T(8,128)(2,1)S(1)} all-to-all(bf16[144,8,256]{2,0,1:T(8,128)(2,1)S(1)} %bitcast.57), channel_id=1, replica_groups=mesh['dp'=32,'seq'=8] {'seq'}, dimensions={1} | all-to-all | bytes 1179648 | tf_op jit(solution)/shard_map/all_to_all | solution.py:78
  76.6 2.4 collective-permute-start
  80.9 4.2 %all-to-all-start = ((bf16[144,8,256]{2,0,1:T(8,128)(2,1)}), bf16[144,8,256]{2,0,1:T(8,128)(2,1)}, u32[]{:S(2)}, u32[]{:S(2)}) async-start(bf16[144,8,256]{2,0,1:T(8,128)(2,1)} %bitcast.47), calls=%async_computation | async-start | bytes 1179648 | tf_op jit(solution)/shard_map/all_to_all | solution.py:78
  85.8 46.2 %collective-permute-done.1 = bf16[1152,512]{1,0:T(8,128)(2,1)S(1)} collective-permute-done((bf16[1152,512]{1,0:T(8,128)(2,1)}, bf16[1152,512]{1,0:T(8,128)(2,1)S(1)}, u32[]{:S(2)}, u32[]{:S(2)}) %collective-permute-start.1) | collective-permute-done | bytes 1179680 | tf_op jit(solution)/shard_map/ppermute | solution.py:89
  131.9 3.3 pad_maximum_fusion
  135.2 14.9 %all-gather.2.cloned.1.call-done = bf16[2048,3072]{1,0:T(8,128)(2,1)} async-done(((bf16[64,3072]{1,0:T(8,128)(2,1)}), bf16[2048,3072]{1,0:T(8,128)(2,1)}) %all-gather.2.cloned.1.call-update) | async-done | bytes 12582928 | tf_op jit(solution)/shard_map/all_gather | solution.py:94
  150.1 8.9 %convolution_convert_fusion.1 = bf16[144,2048]{1,0:T(8,128)(2,1)S(1)} fusion(bf16[144,3072]{1,0:T(8,128)(2,1)S(1)} %copy-done, bf16[2048,3072]{1,0:T(8,128)(2,1)} %all-gather.2.cloned.1.call-done), kind=kOutput, calls=%fused_computation.2 | convolution fusion | flops 1812234240 | bytes 14057472 | tf_op jit(solution)/shard_map/dot_general | solution.py:103
  159.8 8.4 %all-to-all-start.1 = ((bf16[144,8,256]{2,0,1:T(8,128)(2,1)}), bf16[144,8,256]{2,0,1:T(8,128)(2,1)S(1)}, u32[]{:S(2)}, u32[]{:S(2)}) async-start(bf16[144,8,256]{2,0,1:T(8,128)(2,1)} %bitcast.46), calls=%async_computation.1 | async-start | bytes 1179648 | tf_op jit(solution)/shard_map/all_to_all | solution.py:78
  168.2 4.0 %fusion.3 = (bf16[3456,256]{1,0:T(8,128)(2,1)}, bf16[3456,256]{1,0:T(8,128)(2,1)}) fusion(bf16[3456,512]{1,0:T(8,128)(2,1)} %pad_maximum_fusion), kind=kLoop, calls=%fused_computation.15 | loop fusion | bytes 7077888 | tf_op jit(solution)/shard_map/slice | solution.py:107
  172.3 16.6 %all-to-all-done.1 = bf16[144,8,256]{2,0,1:T(8,128)(2,1)S(1)} async-done(((bf16[144,8,256]{2,0,1:T(8,128)(2,1)}), bf16[144,8,256]{2,0,1:T(8,128)(2,1)S(1)}, u32[]{:S(2)}, u32[]{:S(2)}) %all-to-all-start.1) | async-done | bytes 589856 | tf_op jit(solution)/shard_map/all_to_all | solution.py:78
  189.6 25.2 %shard_map.102 = (bf16[1152,256]{1,0:T(8,128)(2,1)}, bf16[1152,256]{1,0:T(8,128)(2,1)}, f32[3456,256]{1,0:T(8,128)}, f32[3456,256]{1,0:T(8,128)}) custom-call(s32[3,5]{1,0:T(4,128)} %broadcast_subtract_fusion.ids, s32[3]{0:T(128)} %counts.1, bf16[1152,256]{1,0:T(8,128)(2,1)} %bitcast.1.q_ref, bf16[1152,256]{1,0:T(8,128)(2,1)} %bitcast.67, ...), custom_call_target="tpu_custom_call" | custom-call | flops 41999998976 | bytes 14000000 | tf_op jit(solution)/shard_map/pallas_call | solution.py:65
  214.8 2.6 constant_dynamic-update-slice_fusion.1
  218.9 2.3 copy-done.1
  224.8 3.6 %collective-permute-start.3 = (bf16[1152,512]{1,0:T(8,128)(2,1)}, bf16[1152,512]{1,0:T(8,128)(2,1)}, u32[]{:S(2)}, u32[]{:S(2)}) collective-permute-start(bf16[1152,512]{1,0:T(8,128)(2,1)} %get-tuple-element.13), channel_id=1, source_target_pairs={{8,0},{16,8},{24,16},{32,24},{40,32},{48,40},{56,48},{64,56},{72,6... | collective-permute-start | bytes 3538952 | tf_op jit(solution)/shard_map/ppermute | solution.py:89
  228.5 40.3 %all_to_all.153 = bf16[8,144,256]{2,1,0:T(8,128)(2,1)S(1)} all-to-all(bf16[8,144,256]{2,1,0:T(8,128)(2,1)S(1)} %bitcast.65), channel_id=1, replica_groups=mesh['dp'=32,'seq'=8] {'seq'}, dimensions={0} | all-to-all | bytes 1179648 | tf_op jit(solution)/shard_map/all_to_all | solution.py:82
  268.8 9.9 %all-to-all-start.4 = ((bf16[8,144,256]{2,1,0:T(8,128)(2,1)}), bf16[8,144,256]{2,1,0:T(8,128)(2,1)S(1)}, u32[]{:S(2)}, u32[]{:S(2)}) async-start(bf16[8,144,256]{2,1,0:T(8,128)(2,1)} %bitcast.64), calls=%async_computation.4 | async-start | bytes 1179648 | tf_op jit(solution)/shard_map/all_to_all | solution.py:82
  278.7 2.5 fusion.1
  282.0 14.1 %all-to-all-done.4 = bf16[8,144,256]{2,1,0:T(8,128)(2,1)S(1)} async-done(((bf16[8,144,256]{2,1,0:T(8,128)(2,1)}), bf16[8,144,256]{2,1,0:T(8,128)(2,1)S(1)}, u32[]{:S(2)}, u32[]{:S(2)}) %all-to-all-start.4) | async-done | bytes 589856 | tf_op jit(solution)/shard_map/all_to_all | solution.py:82
  296.1 20.3 %all_to_all.154 = bf16[8,144,256]{2,1,0:T(8,128)(2,1)S(1)} all-to-all(bf16[8,144,256]{2,1,0:T(8,128)(2,1)S(1)} %bitcast.59), channel_id=1, replica_groups=mesh['dp'=32,'seq'=8] {'seq'}, dimensions={0} | all-to-all | bytes 1179648 | tf_op jit(solution)/shard_map/all_to_all | solution.py:82
  316.5 3.5 %all-to-all-start.7 = ((bf16[8,144,256]{2,1,0:T(8,128)(2,1)}), bf16[8,144,256]{2,1,0:T(8,128)(2,1)S(1)}, u32[]{:S(2)}, u32[]{:S(2)}) async-start(bf16[8,144,256]{2,1,0:T(8,128)(2,1)} %bitcast.58), calls=%async_computation.7 | async-start | bytes 1179648 | tf_op jit(solution)/shard_map/all_to_all | solution.py:82
  321.0 7.5 %convolution_convert_fusion = bf16[144,3072]{1,0:T(8,128)(2,1)} fusion(bf16[144,2048]{1,0:T(8,128)(2,1)S(1)} %bitcast.52, bf16[2048,3072]{1,0:T(8,128)(2,1)} %all-gather.2.cloned.1.call-done), kind=kOutput, calls=%fused_computation | convolution fusion | flops 1812381696 | bytes 14057472 | tf_op jit(solution)/shard_map/dot_general | solution.py:112
  329.4 4.9 %all-to-all-done.7 = bf16[8,144,256]{2,1,0:T(8,128)(2,1)S(1)} async-done(((bf16[8,144,256]{2,1,0:T(8,128)(2,1)}), bf16[8,144,256]{2,1,0:T(8,128)(2,1)S(1)}, u32[]{:S(2)}, u32[]{:S(2)}) %all-to-all-start.7) | async-done | bytes 589856 | tf_op jit(solution)/shard_map/all_to_all | solution.py:82
  (33 shorter events, 19.6 us)
Async XLA Ops:
  7.2 142.9 %copy-start = (bf16[144,3072]{1,0:T(8,128)(2,1)S(1)}, bf16[144,3072]{1,0:T(8,128)(2,1)}, u32[]{:S(2)}) copy-start(bf16[144,3072]{1,0:T(8,128)(2,1)} %param.11) | copy-start | bytes 2654212
  7.2 142.9 %all-gather.2.cloned.1.call-start = ((), (), s32[]{:S(2)}) async-start(), calls=%async_computation.8 | async-start | bytes 12976128 | tf_op jit(solution)/shard_map/all_gather | solution.py:94
  9.8 35.2 %all-to-all-start.2 = ((bf16[144,8,256]{2,0,1:T(8,128)(2,1)}), bf16[144,8,256]{2,0,1:T(8,128)(2,1)S(1)}, u32[]{:S(2)}, u32[]{:S(2)}) async-start(bf16[144,8,256]{2,0,1:T(8,128)(2,1)} %bitcast.45), calls=%async_computation.2 | async-start | bytes 1179648 | tf_op jit(solution)/shard_map/all_to_all | solution.py:78
  19.9 65.3 %copy-start.5 = (s32[3,5]{1,0:T(4,128)S(1)}, s32[3,5]{1,0:T(4,128)}, u32[]{:S(2)}) copy-start(s32[3,5]{1,0:T(4,128)} %param.12) | copy-start | bytes 184
  74.7 57.2 %collective-permute-start.1 = (bf16[1152,512]{1,0:T(8,128)(2,1)}, bf16[1152,512]{1,0:T(8,128)(2,1)S(1)}, u32[]{:S(2)}, u32[]{:S(2)}) collective-permute-start(bf16[1152,512]{1,0:T(8,128)(2,1)} %pad_maximum_fusion.1), channel_id=1, source_target_pairs={{8,0},{16,8},{24,16},{32,24},{40,32},{48,40},{56,48},{64,56},{72,6... | collective-permute-start | bytes 3538952 | tf_op jit(solution)/shard_map/ppermute | solution.py:89
  76.6 55.3 %collective-permute-start = (bf16[1152,512]{1,0:T(8,128)(2,1)}, bf16[1152,512]{1,0:T(8,128)(2,1)}, u32[]{:S(2)}, u32[]{:S(2)}) collective-permute-start(bf16[1152,512]{1,0:T(8,128)(2,1)} %pad_maximum_fusion.1), channel_id=1, source_target_pairs={{0,8},{8,16},{16,24},{24,32},{32,40},{40,48},{48,56},{56,64},{64,7... | collective-permute-start | bytes 3538952 | tf_op jit(solution)/shard_map/ppermute | solution.py:89
  80.9 78.9 %all-to-all-start = ((bf16[144,8,256]{2,0,1:T(8,128)(2,1)}), bf16[144,8,256]{2,0,1:T(8,128)(2,1)}, u32[]{:S(2)}, u32[]{:S(2)}) async-start(bf16[144,8,256]{2,0,1:T(8,128)(2,1)} %bitcast.47), calls=%async_computation | async-start | bytes 1179648 | tf_op jit(solution)/shard_map/all_to_all | solution.py:78
  159.8 29.0 %all-to-all-start.1 = ((bf16[144,8,256]{2,0,1:T(8,128)(2,1)}), bf16[144,8,256]{2,0,1:T(8,128)(2,1)S(1)}, u32[]{:S(2)}, u32[]{:S(2)}) async-start(bf16[144,8,256]{2,0,1:T(8,128)(2,1)} %bitcast.46), calls=%async_computation.1 | async-start | bytes 1179648 | tf_op jit(solution)/shard_map/all_to_all | solution.py:78
  188.8 0.8 copy-start.4
  214.8 3.1 copy-start.2
  218.5 2.8 copy-start.1
  221.3 7.2 %copy-start.3 = (bf16[1152,256]{1,0:T(8,128)(2,1)S(1)}, bf16[1152,256]{1,0:T(8,128)(2,1)}, u32[]{:S(2)}) copy-start(bf16[1152,256]{1,0:T(8,128)(2,1)} %get-tuple-element.9) | copy-start | bytes 1769476
  222.9 55.8 %collective-permute-start.2 = (bf16[1152,512]{1,0:T(8,128)(2,1)}, bf16[1152,512]{1,0:T(8,128)(2,1)S(1)}, u32[]{:S(2)}, u32[]{:S(2)}) collective-permute-start(bf16[1152,512]{1,0:T(8,128)(2,1)} %get-tuple-element.12), channel_id=1, source_target_pairs={{0,8},{8,16},{16,24},{24,32},{32,40},{40,48},{48,56},{56,64},{64,7... | collective-permute-start | bytes 3538952 | tf_op jit(solution)/shard_map/ppermute | solution.py:89
  224.8 53.9 %collective-permute-start.3 = (bf16[1152,512]{1,0:T(8,128)(2,1)}, bf16[1152,512]{1,0:T(8,128)(2,1)}, u32[]{:S(2)}, u32[]{:S(2)}) collective-permute-start(bf16[1152,512]{1,0:T(8,128)(2,1)} %get-tuple-element.13), channel_id=1, source_target_pairs={{8,0},{16,8},{24,16},{32,24},{40,32},{48,40},{56,48},{64,56},{72,6... | collective-permute-start | bytes 3538952 | tf_op jit(solution)/shard_map/ppermute | solution.py:89
  268.8 27.3 %all-to-all-start.4 = ((bf16[8,144,256]{2,1,0:T(8,128)(2,1)}), bf16[8,144,256]{2,1,0:T(8,128)(2,1)S(1)}, u32[]{:S(2)}, u32[]{:S(2)}) async-start(bf16[8,144,256]{2,1,0:T(8,128)(2,1)} %bitcast.64), calls=%async_computation.4 | async-start | bytes 1179648 | tf_op jit(solution)/shard_map/all_to_all | solution.py:82
  316.5 17.8 %all-to-all-start.7 = ((bf16[8,144,256]{2,1,0:T(8,128)(2,1)}), bf16[8,144,256]{2,1,0:T(8,128)(2,1)S(1)}, u32[]{:S(2)}, u32[]{:S(2)}) async-start(bf16[8,144,256]{2,1,0:T(8,128)(2,1)} %bitcast.58), calls=%async_computation.7 | async-start | bytes 1179648 | tf_op jit(solution)/shard_map/all_to_all | solution.py:82
Sparse Core Ops, SparseCore 0:
  9.8 140.2 all-gather.1

commit v2 on v1

v2 whole, which is shorter than its diff:
```python
import jax
import jax.numpy as jnp
from jax import lax
from jax.experimental import pallas as pl
from jax.experimental.pallas import tpu as pltpu
from jax.sharding import PartitionSpec as P

HD = 128
TILE = 384
WIN = 5
LOG2E = 1.4426950408889634
MESH = pl.DeviceIdType.MESH
BF16 = jnp.bfloat16
F32 = jnp.float32


def dotT(a, b):
    return lax.dot_general(a, b, (((1,), (1,)), ((), ())), preferred_element_type=F32)


def dot0(a, b):
    return lax.dot_general(a, b, (((0,), (0,)), ((), ())), preferred_element_type=F32)


def dot(a, b):
    return jnp.dot(a, b, preferred_element_type=F32)


def flip(dp, index):
    return lax.rem(index + 4 * lax.rem(dp // 8, 2), 8)


def ring(index, step, count):
    return lax.rem(index + step + count, count)


def rows_of(index, count):
    return pl.ds(pl.multiple_of(index * count, count), count)


def pair_columns(pair):
    return pl.ds(pl.multiple_of(pair * 256, 256), 256)


def remote(src, dst, send, recv, device):
    return pltpu.make_async_remote_copy(
        src_ref=src, dst_ref=dst, send_sem=send, recv_sem=recv, device_id=device, device_id_type=MESH
    )


def greet(partners):
    barrier = pltpu.get_barrier_semaphore()
    for device in partners:
        pl.semaphore_signal(barrier, inc=1, device_id=device, device_id_type=MESH)
    pl.semaphore_wait(barrier, len(partners))


SIDES = ((-1, 2), (1, 0))


def collect(q_ref, k_ref, v_ref, w_ref, og_ref, q_out, k_out, v_out, g_out, w_out,
            g_stage, w_buf, a_send, a_recv, h_send, h_recv, g_send, g_recv,
            wz_send, wz_recv, wx_send, wx_recv, wy_send, wy_recv, wq_send, wq_recv,
            wxx_send, wxx_recv, sib_send, sib_recv, own_sem, load_sem):
    dp = lax.axis_index("dp")
    seq = lax.axis_index("seq")
    y, z_lo, core = dp // 8, lax.rem(dp // 2, 4), lax.rem(dp, 2)
    x = lax.rem(seq, 4)
    z = (seq // 4) * 4 + z_lo
    pair = flip(dp, seq)
    tokens = q_ref.shape[0]
    share = w_ref.shape[0]
    quarter = share // 4

    def along_z(step):
        to = lax.rem(z + step + 8, 8)
        return (y * 8 + lax.rem(to, 4) * 2 + core, (to // 4) * 4 + x)

    def along_y(step):
        return (lax.rem(y + step + 4, 4) * 8 + lax.rem(dp, 8), seq)

    def along_x(step):
        return (dp, (seq // 4) * 4 + lax.rem(x + step + 4, 4))

    sibling = (dp + 1 - 2 * core, seq)
    far = 2 - 4 * core
    beside = [(ring(dp, step, 32), flip(ring(dp, step, 32), pair)) for step, _ in SIDES]
    greet([(dp, ring(seq, r, 8)) for r in range(1, 8)] + beside
          + [along_z(1), along_z(-1), along_z(2), along_z(-2)]
          + [along_y(1), along_y(-1), along_y(2), sibling])

    z_off = (0, -1, 1, 2)
    y_off = (0, -1, 1, 2)

    def shard(o, i, mine=True):
        c = core if mine else 1 - core
        return lax.rem(y + y_off[o] + 4, 4) * 8 + lax.rem(z_lo + z_off[i] + 4, 4) * 2 + c

    def whole(o, i, mine=True):
        return w_out.at[rows_of(shard(o, i, mine), share), :]

    def part(o, i, of_x):
        return w_out.at[rows_of(shard(o, i) * 4 + of_x, quarter), :]

    def x_from(j):
        return lax.rem(x - j + 4, 4)

    own_quarter = w_ref.at[rows_of(x, quarter), :]
    pending = []

    def go(copy):
        copy.start()
        pending.append(copy)

    def send_z(i, step):
        return remote(own_quarter, part(0, 0, x), wz_send.at[i], wz_recv.at[i], along_z(step))

    def got_z(i):
        return remote(own_quarter, part(0, i + 1, x), wz_send.at[i], wz_recv.at[i], along_z(1))

    go(send_z(0, 1))
    go(send_z(1, -1))
    go(send_z(2, far))

    def send_y(i, src):
        go(remote(src, whole(0, i), wy_send.at[0, i], wy_recv.at[0, i], along_y(1)))
        go(remote(src, whole(0, i), wy_send.at[1, i], wy_recv.at[1, i], along_y(-1)))

    def send_sibling(o, i, src):
        go(remote(src, whole(o, i), sib_send.at[o * 4 + i], sib_recv.at[o * 4 + i], sibling))

    def send_across(i, src):
        go(remote(src, part(0, i, x), wq_send.at[i], wq_recv.at[i], along_y(2)))

    send_across(0, own_quarter)
    send_y(0, w_ref)
    send_sibling(0, 0, w_ref)
    keep = pltpu.make_async_copy(w_ref, whole(0, 0), own_sem.at[3])
    keep.start()

    ext = 8 * tokens

    def landing(out, index, place):
        if place is None:
            return out.at[rows_of(index, tokens), :]
        return out.at[pl.ds(pl.multiple_of(place * ext + index * tokens, tokens), tokens), :]

    sources = ((k_ref, k_out, 1), (v_ref, v_out, 1), (q_ref, q_out, None))

    def exchange(n, r):
        ref, out, place = sources[n]
        to = ring(seq, r, 8)
        block = ref.at[:, pair_columns(flip(dp, to))]
        return remote(block, landing(out, seq, place), a_send.at[n, r], a_recv.at[n, r], (dp, to))

    def arrival(n, r):
        ref, out, place = sources[n]
        src = ring(seq, -r, 8)
        return remote(ref.at[:, pair_columns(pair)], landing(out, src, place), a_send.at[n, r],
                      a_recv.at[n, r], (dp, src))

    def pass_on(n, r, src):
        _, out, _ = sources[n]
        index = ring(seq, -r, 8)
        for side in range(2):
            go(remote(src, landing(out, index, SIDES[side][1]), h_send.at[side, n, r],
                      h_recv.at[side, n, r], beside[side]))

    def passed(n, r, side):
        out = sources[n][1]
        index = ring(flip(beside[side][0], pair), -r, 8)
        return remote(out.at[pl.ds(0, tokens), :], landing(out, index, SIDES[1 - side][1]),
                      h_send.at[1 - side, n, r], h_recv.at[1 - side, n, r], beside[side])

    far_first = (4, 3, 5, 2, 6, 1, 7)
    keeps = [keep]
    for n in range(3):
        ref, out, place = sources[n]
        mine = pltpu.make_async_copy(ref.at[:, pair_columns(pair)], landing(out, seq, place), own_sem.at[n])
        mine.start()
        keeps.append(mine)
    for n in range(2):
        for r in far_first:
            go(exchange(n, r))
    for n in range(2):
        pass_on(n, 0, sources[n][0].at[:, pair_columns(pair)])
    for r in far_first:
        go(exchange(2, r))

    for i in range(3):
        got_z(i).wait_recv()
        piece = part(0, i + 1, x)
        for j in range(1, 4):
            go(remote(piece, piece, wx_send.at[i, j - 1], wx_recv.at[i, j - 1], along_x(j)))
        send_across(i + 1, piece)
    for r in (1, 7):
        for n in range(2):
            arrival(n, r).wait_recv()
            pass_on(n, r, landing(sources[n][1], ring(seq, -r, 8), 1))
    for i in range(3):
        for j in range(1, 4):
            piece = part(0, i + 1, x_from(j))
            remote(piece, piece, wx_send.at[i, j - 1], wx_recv.at[i, j - 1], along_x(-j)).wait_recv()
        send_y(i + 1, whole(0, i + 1))
        send_sibling(0, i + 1, whole(0, i + 1))
    for r in (4, 3, 5, 2, 6):
        for n in range(2):
            arrival(n, r).wait_recv()
            pass_on(n, r, landing(sources[n][1], ring(seq, -r, 8), 1))
    for i in range(4):
        piece = part(3, i, x)
        remote(piece, piece, wq_send.at[i], wq_recv.at[i], along_y(2)).wait_recv()
        for j in range(1, 4):
            go(remote(piece, piece, wxx_send.at[i, j - 1], wxx_recv.at[i, j - 1], along_x(j)))
        for o in (1, 2):
            block = whole(o, i)
            remote(block, block, wy_send.at[o - 1, i], wy_recv.at[o - 1, i], along_y(y_off[o])).wait_recv()
            send_sibling(o, i, block)

    grads = []

    def project(o):
        for i in range(4):
            block = whole(o, i, False)
            remote(block, block, sib_send.at[o * 4 + i], sib_recv.at[o * 4 + i], sibling).wait_recv()
        base = 2 * lax.rem(y + y_off[o] + 4, 4)
        loads = [pltpu.make_async_copy(w_out.at[rows_of(base + b, 256), :], w_buf.at[b], load_sem.at[b])
                 for b in range(2)]
        for load in loads:
            load.start()
        for b in range(2):
            loads[b].wait()
            g_stage[2 * o + b] = dotT(og_ref[...], w_buf[b]).astype(BF16)
        for b in range(2):
            to = flip(dp, base + b)

            @pl.when(to != seq)
            def _():
                remote(g_stage.at[2 * o + b], g_out.at[rows_of(seq, tokens), :], g_send.at[2 * o + b],
                       g_recv.at[seq], (dp, to)).start()

            @pl.when(to == seq)
            def _():
                pltpu.make_async_copy(g_stage.at[2 * o + b], g_out.at[rows_of(seq, tokens), :], g_send.at[2 * o + b]).start()

            grads.append((2 * o + b, to))

    keep.wait()
    keeps.pop(0)
    project(0)
    for i in range(4):
        for j in range(1, 4):
            piece = part(3, i, x_from(j))
            remote(piece, piece, wxx_send.at[i, j - 1], wxx_recv.at[i, j - 1], along_x(-j)).wait_recv()
        send_sibling(3, i, whole(3, i))
    project(1)
    project(2)
    project(3)

    for copy in keeps:
        copy.wait()
    for r in far_first:
        arrival(2, r).wait_recv()
    for n in range(2):
        for r in range(8):
            for side in range(2):
                passed(n, r, side).wait_recv()
    for r in range(1, 8):
        src = ring(seq, -r, 8)
        remote(g_stage.at[0], g_out.at[rows_of(src, tokens), :], g_send.at[0], g_recv.at[src], (dp, src)).wait_recv()
    for slot, to in grads:

        @pl.when(to != seq)
        def _():
            remote(g_stage.at[slot], g_out.at[rows_of(seq, tokens), :], g_send.at[slot], g_recv.at[seq],
                   (dp, to)).wait_send()

        @pl.when(to == seq)
        def _():
            pltpu.make_async_copy(g_stage.at[slot], g_out.at[rows_of(seq, tokens), :], g_send.at[slot]).wait()
    for copy in pending:
        copy.wait_send()


def gather(query, key_in, value, out_weight, out_grad):
    tokens, width = query.shape
    rows = 8 * tokens
    vm = pl.BlockSpec(memory_space=pltpu.VMEM)
    hbm = pl.BlockSpec(memory_space=pl.ANY)
    sem = pltpu.SemaphoreType.DMA
    slab = jax.ShapeDtypeStruct((rows, 256), BF16)
    three = jax.ShapeDtypeStruct((3 * rows, 256), BF16)
    pairs = [(3, 8), (2, 2, 8), (8,), (3,), (3, 3), (2, 4), (4,), (4, 3), (16,)]
    return pl.pallas_call(
        collect,
        out_shape=[slab, three, three, slab, jax.ShapeDtypeStruct((32 * out_weight.shape[0], out_weight.shape[1]), BF16)],
        in_specs=[vm] * 5,
        out_specs=[hbm] * 5,
        scratch_shapes=[pltpu.VMEM((8, tokens, 256), BF16), pltpu.VMEM((2, 256, out_weight.shape[1]), BF16)]
        + [sem(p) for p in pairs for _ in range(2)] + [sem((4,)), sem((2,))],
        compiler_params=pltpu.CompilerParams(collective_id=0, has_side_effects=True, vmem_limit_bytes=40 << 20),
    )(query, key_in, value, out_weight, out_grad)


def deliver(attn_ref, dq_ref, dk_ref, dv_ref, rk_ref, rv_ref, w_ref, o_out, q_out, k_out, v_out,
            tok, own, low, high, stage, w_buf, a_send, a_recv, q_send, q_recv, h_send, h_recv,
            s_send, s_recv, own_sem, w_sem, f_sem):
    dp = lax.axis_index("dp")
    seq = lax.axis_index("seq")
    pair = flip(dp, seq)
    tokens = o_out.shape[0]
    beside = [(ring(dp, step, 32), flip(ring(dp, step, 32), pair)) for step, _ in SIDES]
    loads = [pltpu.make_async_copy((dk_ref, dv_ref)[n], own.at[n], f_sem.at[n]) for n in range(2)]
    for load in loads:
        load.start()
    cut = w_buf.shape[2]
    chunks = [pltpu.make_async_copy(w_ref.at[:, pl.ds(c * cut, cut)], w_buf.at[c], w_sem.at[c])
              for c in range(w_buf.shape[0])]
    greet([(dp, ring(seq, r, 8)) for r in range(1, 8)] + beside)
    pending = []

    def go(copy):
        copy.start()
        pending.append(copy)

    rims = (rk_ref, rv_ref)
    far_first = (4, 3, 5, 2, 6, 1, 7, 0)
    into = (high, low)

    def rim(n, r, side):
        index = ring(seq, r, 8)
        return remote(rims[n].at[side, rows_of(index, tokens), :], into[side].at[n, rows_of(index, tokens), :],
                      h_send.at[side, n, index], h_recv.at[side, n, index], beside[side])

    for r in far_first:
        for n in range(2):
            for side in range(2):
                go(rim(n, r, side))

    def tokens_at(index):
        return rows_of(index, tokens)

    for r in far_first[:-1]:
        to = ring(seq, r, 8)
        go(remote(attn_ref.at[tokens_at(to), :], tok.at[:, pair_columns(pair)], a_send.at[r], a_recv.at[r], (dp, to)))
    for r in far_first[:-1]:
        to = ring(seq, r, 8)
        go(remote(dq_ref.at[tokens_at(to), :], q_out.at[:, pair_columns(pair)], q_send.at[r], q_recv.at[r], (dp, to)))
    keeps = [pltpu.make_async_copy(attn_ref.at[tokens_at(seq), :], tok.at[:, pair_columns(pair)], own_sem.at[0]),
             pltpu.make_async_copy(dq_ref.at[tokens_at(seq), :], q_out.at[:, pair_columns(pair)], own_sem.at[1])]
    for copy in keeps:
        copy.start()
    for chunk in chunks:
        chunk.start()
    for load in loads:
        load.wait()
    outs = (k_out, v_out)

    def send_sum(r):
        to = ring(seq, r, 8)
        for n in range(2):
            if r:
                go(remote(stage.at[n, tokens_at(to), :], outs[n].at[:, pair_columns(pair)], s_send.at[n, r],
                          s_recv.at[n, r], (dp, to)))
            else:
                copy = pltpu.make_async_copy(stage.at[n, tokens_at(to), :], outs[n].at[:, pair_columns(pair)], own_sem.at[2 + n])
                copy.start()
                keeps.append(copy)

    last = None
    for r in far_first:
        index = ring(seq, r, 8)
        at = tokens_at(index)
        for n in range(2):
            for side in range(2):
                remote(rims[n].at[side, at, :], into[side].at[n, at, :], h_send.at[side, n, index],
                       h_recv.at[side, n, index], beside[1 - side]).wait_recv()
            stage[n, at, :] = (own[n, at, :] + low[n, at, :].astype(F32) + high[n, at, :].astype(F32)).astype(BF16)
        if last is not None:
            send_sum(last)
        last = r
    send_sum(last)

    keeps[0].wait()
    keeps.pop(0)
    for r in far_first[:-1]:
        src = ring(seq, -r, 8)
        remote(attn_ref.at[tokens_at(src), :], tok.at[:, pair_columns(flip(dp, src))], a_send.at[r], a_recv.at[r], (dp, src)).wait_recv()
    for c in range(len(chunks)):
        chunks[c].wait()
        o_out[:, c * cut:(c + 1) * cut] = dot(tok[...], w_buf[c]).astype(BF16)
    for copy in keeps:
        copy.wait()
    for r in far_first[:-1]:
        src = ring(seq, -r, 8)
        columns = pair_columns(flip(dp, src))
        remote(dq_ref.at[tokens_at(src), :], q_out.at[:, columns], q_send.at[r], q_recv.at[r], (dp, src)).wait_recv()
        for n in range(2):
            remote(stage.at[n, tokens_at(src), :], outs[n].at[:, columns], s_send.at[n, r], s_recv.at[n, r], (dp, src)).wait_recv()
    for copy in pending:
        copy.wait_send()


def scatter(attn, dq, dk, dv, rk, rv, weight):
    rows, width = attn.shape
    tokens = rows // 8
    depth = weight.shape[1]
    vm = pl.BlockSpec(memory_space=pltpu.VMEM)
    hbm = pl.BlockSpec(memory_space=pl.ANY)
    sem = pltpu.SemaphoreType.DMA
    wide = jax.ShapeDtypeStruct((tokens, 8 * width), BF16)
    cut = 512
    pairs = [(8,), (8,), (2, 2, 8), (2, 8)]
    return pl.pallas_call(
        deliver,
        out_shape=[jax.ShapeDtypeStruct((tokens, depth), BF16), wide, wide, wide],
        in_specs=[hbm] * 7,
        out_specs=[vm] * 4,
        scratch_shapes=[
            pltpu.VMEM((tokens, 8 * width), BF16), pltpu.VMEM((2, rows, width), F32), pltpu.VMEM((2, rows, width), BF16),
            pltpu.VMEM((2, rows, width), BF16), pltpu.VMEM((2, rows, width), BF16), pltpu.VMEM((depth // cut, weight.shape[0], cut), BF16)]
        + [sem(p) for p in pairs for _ in range(2)] + [sem((4,)), sem((depth // cut,)), sem((2,))],
        compiler_params=pltpu.CompilerParams(collective_id=1, has_side_effects=True, vmem_limit_bytes=48 << 20),
    )(attn, dq, dk, dv, rk, rv, weight)


def attend(ids, counts, q_ref, g_ref, k_ref, v_ref, attn_ref, dq_ref, dk_out, dv_out, rk_out, rv_out,
           s_buf, e_buf, dk_ref, dv_ref):
    factor = HD ** -0.5
    t = pl.program_id(1)
    @pl.when(t == 0)
    def _():
        dk_ref[...] = jnp.zeros_like(dk_ref)
        dv_ref[...] = jnp.zeros_like(dv_ref)
    q = q_ref[...]; g = g_ref[...]
    count = counts[t]
    top = None
    for j in range(WIN):
        rows = pl.ds(pl.multiple_of(ids[t, j] * TILE, TILE), TILE)
        s = dotT(q, k_ref[rows, :])
        if j > 0:
            s = s + jnp.where(j < count, 0.0, -jnp.inf).astype(jnp.float32)
        s_buf[j] = s
        m = jnp.max(s, axis=1, keepdims=True)
        top = m if top is None else jnp.maximum(top, m)
    total = jnp.zeros((TILE, 1), jnp.float32)
    acc = jnp.zeros((TILE, HD), jnp.float32)
    for j in range(WIN):
        rows = pl.ds(pl.multiple_of(ids[t, j] * TILE, TILE), TILE)
        e = jnp.exp2((s_buf[j] - top) * (factor * LOG2E))
        total = total + jnp.sum(e, axis=1, keepdims=True)
        eb = e.astype(jnp.bfloat16)
        e_buf[j] = eb
        acc = acc + dot(eb, v_ref[rows, :])
    inv = 1.0 / total
    attn = acc * inv
    attn_ref[...] = attn.astype(jnp.bfloat16)
    gf = g.astype(jnp.float32)
    centre = jnp.sum(gf * attn, axis=1, keepdims=True)
    gs = (gf * inv).astype(jnp.bfloat16)
    qs = (q.astype(jnp.float32) * (inv * factor)).astype(jnp.bfloat16)
    dq = jnp.zeros((TILE, HD), jnp.float32)
    for j in range(WIN):
        rows = pl.ds(pl.multiple_of(ids[t, j] * TILE, TILE), TILE)
        dp = dotT(g, v_ref[rows, :])
        eb = e_buf[j]
        ds = (eb.astype(jnp.float32) * (dp - centre)).astype(jnp.bfloat16)
        dq = dq + dot(ds, k_ref[rows, :])
        dk_ref[rows, :] += dot0(ds, qs)
        dv_ref[rows, :] += dot0(eb, gs)
    dq_ref[...] = (dq * (inv * factor)).astype(jnp.bfloat16)

    @pl.when(t == pl.num_programs(1) - 1)
    def _():
        n = dk_out.shape[0]
        for acc_ref, own, rim in ((dk_ref, dk_out, rk_out), (dv_ref, dv_out, rv_out)):
            rim[0] = acc_ref[:n, :].astype(jnp.bfloat16)
            own[...] = acc_ref[n:2 * n, :]
            rim[1] = acc_ref[2 * n:, :].astype(jnp.bfloat16)

def attention(q, g, k, v, ids, counts):
    rows, width = q.shape
    ext = k.shape[0]
    heads = width // HD
    tiles = rows // TILE
    qs = pl.BlockSpec((TILE, HD), lambda h, t, *_: (t, h))
    ks = pl.BlockSpec((ext, HD), lambda h, t, *_: (0, h))
    own = pl.BlockSpec((rows, HD), lambda h, t, *_: (0, h))
    rim = pl.BlockSpec((2, rows, HD), lambda h, t, *_: (0, 0, h))
    bf = jax.ShapeDtypeStruct((rows, width), jnp.bfloat16)
    f32 = jax.ShapeDtypeStruct((rows, width), jnp.float32)
    rims = jax.ShapeDtypeStruct((2, rows, width), jnp.bfloat16)
    return pl.pallas_call(
        attend,
        grid_spec=pltpu.PrefetchScalarGridSpec(
            num_scalar_prefetch=2, grid=(heads, tiles),
            in_specs=[qs, qs, ks, ks], out_specs=[qs, qs, own, own, rim, rim],
            scratch_shapes=[pltpu.VMEM((WIN, TILE, TILE), jnp.float32), pltpu.VMEM((WIN, TILE, TILE), jnp.bfloat16),
                            pltpu.VMEM((ext, HD), jnp.float32), pltpu.VMEM((ext, HD), jnp.float32)]),
        out_shape=[bf, bf, f32, f32, rims, rims],
        compiler_params=pltpu.CompilerParams(vmem_limit_bytes=60 << 20),
    )(ids, counts, q, g, k, v)


def body(query, key_in, value, out_weight, out_grad, windows, window_count):
    q, k, v, g, weight = gather(query, key_in, value, out_weight, out_grad)
    ids = windows - (lax.axis_index("dp") - 1) * windows.shape[0]
    attn, dq, dk, dv, rk, rv = attention(q, g, k, v, ids, window_count)
    return tuple(scatter(attn, dq, dk, dv, rk, rv, weight))


def solution(mesh):
    both = P(("dp", "seq"), None)
    return jax.shard_map(
        body, mesh=mesh, check_vma=False,
        in_specs=(both, both, both, P("dp", None), both, P("dp", None), P("dp")),
        out_specs=(both, both, both, both),
    )
```

time: 343 us -> 227 us (0.66)
  the two profiles are of different devices: /device:TPU:32 before, /device:TPU:14 now
where the time goes in v2:
time: 227 us
  Pallas kernels  207 us (91%)
  local copies, waits for them, and re-layouts  17.5 us (8%)
    pallas_call x1, Pallas kernels, gather(): pl.pallas_call(collect, out_shape=[slab, three, three, slab, jax.ShapeDty...  99 us
    pallas_call x1, Pallas kernels, scatter(): pl.pallas_call(deliver, out_shape=[jax.ShapeDtypeStruct((tokens, depth),...  82.8 us
    pallas_call x1, Pallas kernels, attention(): pl.pallas_call(attend, grid_spec=pltpu.PrefetchScalarGridSpec(num_scalar_...  25.4 us
    unnamed x30, local copies, waits for them, and re-layouts  17.5 us

profile of v2, /device:TPU:14, one launch (start us, length us, event | category | flops | bytes accessed | tf_op | source)
XLA Modules:
  0.0 226.6 jit_solution(11449109670344096125)
XLA Ops:
  0.6 1.3 broadcast_subtract_fusion.ids
  1.9 0.0 copy-start.4
  1.9 1.2 copy-done.4
  3.1 0.0 copy-start.9
  3.1 1.1 copy-done.9
  4.1 1.1 copy-done.10
  5.2 1.1 copy-done.11
  6.3 1.0 copy-done.12
  7.3 99.0 %shard_map.102 = (bf16[1152,256]{1,0:T(8,128)(2,1)S(1)}, bf16[3456,256]{1,0:T(8,128)(2,1)S(1)}, bf16[3456,256]{1,0:T(8,128)(2,1)S(1)}, bf16[1152,256]{1,0:T(8,128)(2,1)S(1)}, bf16[2048,3072]{1,0:T(8,128)(2,1)}) custom-call(bf16[144,2048]{1,0:T(8,128)(2,1)S(1)} %copy-done.9, bf16[144,2048]{1,0:T(8,128)(2,1)S(1)} %copy-done.10, ...), custom_call_target="tpu_custom_call" | custom-call | tf_op jit(solution)/shard_map/pallas_call | solution.py:294
  106.3 0.0 copy-start
  106.3 1.2 copy-done
  107.5 1.2 copy-done.1
  108.7 0.8 copy-done.7
  109.5 0.8 copy-done.8
  110.4 25.4 %shard_map.103 = (bf16[1152,256]{1,0:T(8,128)(2,1)}, bf16[1152,256]{1,0:T(8,128)(2,1)}, f32[1152,256]{1,0:T(8,128)}, f32[1152,256]{1,0:T(8,128)}, bf16[2,1152,25...) custom-call(s32[3,5]{1,0:T(4,128)} %broadcast_subtract_fusion.ids, s32[3]{0:T(128)} %counts.1, ...), custom_call_target="tpu_custom_call" | custom-call | tf_op jit(solution)/shard_map/pallas_call | solution.py:493
  135.8 1.3 copy-done.2
  137.1 1.3 copy-done.3
  138.4 1.1 copy-done.5
  139.4 1.1 copy-done.6
  140.5 82.8 %shard_map.104 = (bf16[144,3072]{1,0:T(8,128)(2,1)S(1)}, bf16[144,2048]{1,0:T(8,128)(2,1)S(1)}, bf16[144,2048]{1,0:T(8,128)(2,1)S(1)}, bf16[144,2048]{1,0:T(8,128)(2,1)S(1)}) custom-call(bf16[1152,256]{1,0:T(8,128)(2,1)S(1)} %copy-done.5, bf16[1152,256]{1,0:T(8,128)(2,1)S(1)} %copy-done.6, f32[1152,256]{1,0:T(8,128)S(1)} %copy-done.2, ...), custom_call_target="tpu_custom_call" | custom-call | tf_op jit(solution)/shard_map/pallas_call | solution.py:414
  223.3 0.9 copy.15
  224.2 0.8 copy.16
  225.0 0.8 copy.17
  225.8 0.8 copy.18
  (10 shorter events, 0.0 us)
Async XLA Ops:
  1.9 1.2 copy-start.4
  3.1 1.1 copy-start.9
  4.1 1.1 copy-start.10
  5.2 1.1 copy-start.11
  6.3 1.0 copy-start.12
  106.3 1.2 copy-start
  107.5 1.2 copy-start.1
  108.7 0.8 copy-start.7
  109.5 0.8 copy-start.8
  135.8 1.3 copy-start.2
  137.1 1.3 copy-start.3
  138.3 1.1 copy-start.5
  139.4 1.1 copy-start.6

commit v3 on v2

v3 whole, which is shorter than its diff:
```python
import jax
import jax.numpy as jnp
from jax import lax
from jax.experimental import pallas as pl
from jax.experimental.pallas import tpu as pltpu
from jax.sharding import PartitionSpec as P

HD = 128
TILE = 384
WIN = 5
LOG2E = 1.4426950408889634
MESH = pl.DeviceIdType.MESH
BF16 = jnp.bfloat16
F32 = jnp.float32


def dotT(a, b):
    return lax.dot_general(a, b, (((1,), (1,)), ((), ())), preferred_element_type=F32)


def dot0(a, b):
    return lax.dot_general(a, b, (((0,), (0,)), ((), ())), preferred_element_type=F32)


def dot(a, b):
    return jnp.dot(a, b, preferred_element_type=F32)


def flip(dp, index):
    return lax.rem(index + 4 * lax.rem(dp // 8, 2), 8)


def ring(index, step, count):
    return lax.rem(index + step + count, count)


def rows_of(index, count):
    return pl.ds(pl.multiple_of(index * count, count), count)


def pair_columns(pair):
    return pl.ds(pl.multiple_of(pair * 256, 256), 256)


def remote(src, dst, send, recv, device):
    return pltpu.make_async_remote_copy(
        src_ref=src, dst_ref=dst, send_sem=send, recv_sem=recv, device_id=device, device_id_type=MESH
    )


def greet(partners):
    barrier = pltpu.get_barrier_semaphore()
    for device in partners:
        pl.semaphore_signal(barrier, inc=1, device_id=device, device_id_type=MESH)
    pl.semaphore_wait(barrier, len(partners))


SIDES = ((-1, 2), (1, 0))


def layer(win_ref, count_ref, q_ref, k_ref, v_ref, w_ref, og_in, o_out, dq_out, dk_out, dv_out,
          q_buf, k_out, v_out, g_out, w_out, og_ref, g_stage, s_buf, e_buf, attn_f, inv_f, attn_b, dq_b,
          pieces, own, k_tile, v_tile, rim_buf, low, high, stage, tok,
          a_send, a_recv, h_send, h_recv, g_send, g_recv,
          wz_send, wz_recv, wx_send, wx_recv, wy_send, wy_recv, wq_send, wq_recv,
          wxx_send, wxx_recv, sib_send, sib_recv, t_send, t_recv, d_send, d_recv, r_send, r_recv,
          s_send, s_recv, own_sem):
    dp = lax.axis_index("dp")
    seq = lax.axis_index("seq")
    y, z_lo, core = dp // 8, lax.rem(dp // 2, 4), lax.rem(dp, 2)
    x = lax.rem(seq, 4)
    z = (seq // 4) * 4 + z_lo
    pair = flip(dp, seq)
    tokens = q_ref.shape[0]
    share = w_ref.shape[0]
    quarter = share // 4

    def along_z(step):
        to = lax.rem(z + step + 8, 8)
        return (y * 8 + lax.rem(to, 4) * 2 + core, (to // 4) * 4 + x)

    def along_y(step):
        return (lax.rem(y + step + 4, 4) * 8 + lax.rem(dp, 8), seq)

    def along_x(step):
        return (dp, (seq // 4) * 4 + lax.rem(x + step + 4, 4))

    sibling = (dp + 1 - 2 * core, seq)
    far = 2 - 4 * core
    beside = [(ring(dp, step, 32), flip(ring(dp, step, 32), pair)) for step, _ in SIDES]
    greet([(dp, ring(seq, r, 8)) for r in range(1, 8)] + beside
          + [along_z(1), along_z(-1), along_z(2), along_z(-2)]
          + [along_y(1), along_y(-1), along_y(2), sibling])

    z_off = (0, -1, 1, 2)
    y_off = (0, -1, 1, 2)

    def shard(o, i, mine=True):
        c = core if mine else 1 - core
        return lax.rem(y + y_off[o] + 4, 4) * 8 + lax.rem(z_lo + z_off[i] + 4, 4) * 2 + c

    def whole(o, i, mine=True):
        return w_out.at[rows_of(shard(o, i, mine), share), :]

    def part(o, i, of_x):
        return w_out.at[rows_of(shard(o, i) * 4 + of_x, quarter), :]

    def x_from(j):
        return lax.rem(x - j + 4, 4)

    og_load = pltpu.make_async_copy(og_in, og_ref, own_sem.at[4])
    og_load.start()
    own_quarter = w_ref.at[rows_of(x, quarter), :]
    pending = []

    def go(copy):
        copy.start()
        pending.append(copy)

    def send_z(i, step):
        return remote(own_quarter, part(0, 0, x), wz_send.at[i], wz_recv.at[i], along_z(step))

    def got_z(i):
        return remote(own_quarter, part(0, i + 1, x), wz_send.at[i], wz_recv.at[i], along_z(1))

    go(send_z(0, 1))
    go(send_z(1, -1))
    go(send_z(2, far))

    def send_y(i, src):
        go(remote(src, whole(0, i), wy_send.at[0, i], wy_recv.at[0, i], along_y(1)))
        go(remote(src, whole(0, i), wy_send.at[1, i], wy_recv.at[1, i], along_y(-1)))

    def send_sibling(o, i, src):
        go(remote(src, whole(o, i), sib_send.at[o * 4 + i], sib_recv.at[o * 4 + i], sibling))

    def send_across(i, src):
        go(remote(src, part(0, i, x), wq_send.at[i], wq_recv.at[i], along_y(2)))

    send_across(0, own_quarter)
    send_y(0, w_ref)
    send_sibling(0, 0, w_ref)
    keep = pltpu.make_async_copy(w_ref, whole(0, 0), own_sem.at[3])
    keep.start()

    ext = 8 * tokens

    def landing(out, index, place):
        if place is None:
            return out.at[rows_of(index, tokens), :]
        return out.at[pl.ds(pl.multiple_of(place * ext + index * tokens, tokens), tokens), :]

    sources = ((k_ref, k_out, 1), (v_ref, v_out, 1), (q_ref, q_buf, None))

    def exchange(n, r):
        ref, out, place = sources[n]
        to = ring(seq, r, 8)
        block = ref.at[:, pair_columns(flip(dp, to))]
        return remote(block, landing(out, seq, place), a_send.at[n, r], a_recv.at[n, r], (dp, to))

    def arrival(n, r):
        ref, out, place = sources[n]
        src = ring(seq, -r, 8)
        return remote(ref.at[:, pair_columns(pair)], landing(out, src, place), a_send.at[n, r],
                      a_recv.at[n, r], (dp, src))

    def pass_on(n, r, src):
        _, out, _ = sources[n]
        index = ring(seq, -r, 8)
        for side in range(2):
            go(remote(src, landing(out, index, SIDES[side][1]), h_send.at[side, n, r],
                      h_recv.at[side, n, r], beside[side]))

    def passed(n, r, side):
        out = sources[n][1]
        index = ring(flip(beside[side][0], pair), -r, 8)
        return remote(out.at[pl.ds(0, tokens), :], landing(out, index, SIDES[1 - side][1]),
                      h_send.at[1 - side, n, r], h_recv.at[1 - side, n, r], beside[side])

    far_first = (4, 3, 5, 2, 6, 1, 7)
    keeps = [keep]
    for n in range(3):
        ref, out, place = sources[n]
        mine = pltpu.make_async_copy(ref.at[:, pair_columns(pair)], landing(out, seq, place), own_sem.at[n])
        mine.start()
        keeps.append(mine)
    for n in range(2):
        for r in far_first:
            go(exchange(n, r))
    for n in range(2):
        pass_on(n, 0, sources[n][0].at[:, pair_columns(pair)])
    for r in far_first:
        go(exchange(2, r))

    for i in range(3):
        got_z(i).wait_recv()
        piece = part(0, i + 1, x)
        for j in range(1, 4):
            go(remote(piece, piece, wx_send.at[i, j - 1], wx_recv.at[i, j - 1], along_x(j)))
        send_across(i + 1, piece)
    for r in (1, 7):
        for n in range(2):
            arrival(n, r).wait_recv()
            pass_on(n, r, landing(sources[n][1], ring(seq, -r, 8), 1))
    for i in range(3):
        for j in range(1, 4):
            piece = part(0, i + 1, x_from(j))
            remote(piece, piece, wx_send.at[i, j - 1], wx_recv.at[i, j - 1], along_x(-j)).wait_recv()
        send_y(i + 1, whole(0, i + 1))
        send_sibling(0, i + 1, whole(0, i + 1))
    for r in (4, 3, 5, 2, 6):
        for n in range(2):
            arrival(n, r).wait_recv()
            pass_on(n, r, landing(sources[n][1], ring(seq, -r, 8), 1))
    for i in range(4):
        piece = part(3, i, x)
        remote(piece, piece, wq_send.at[i], wq_recv.at[i], along_y(2)).wait_recv()
        for j in range(1, 4):
            go(remote(piece, piece, wxx_send.at[i, j - 1], wxx_recv.at[i, j - 1], along_x(j)))
        for o in (1, 2):
            block = whole(o, i)
            remote(block, block, wy_send.at[o - 1, i], wy_recv.at[o - 1, i], along_y(y_off[o])).wait_recv()
            send_sibling(o, i, block)

    grads = []

    def project(o):
        for i in range(4):
            block = whole(o, i, False)
            remote(block, block, sib_send.at[o * 4 + i], sib_recv.at[o * 4 + i], sibling).wait_recv()
        base = 2 * lax.rem(y + y_off[o] + 4, 4)
        for b in range(2):
            g_stage[2 * o + b] = dotT(og_ref[...], w_out[rows_of(base + b, 256), :]).astype(BF16)
        for b in range(2):
            to = flip(dp, base + b)

            @pl.when(to != seq)
            def _():
                remote(g_stage.at[2 * o + b], g_out.at[rows_of(seq, tokens), :], g_send.at[2 * o + b],
                       g_recv.at[seq], (dp, to)).start()

            @pl.when(to == seq)
            def _():
                pltpu.make_async_copy(g_stage.at[2 * o + b], g_out.at[rows_of(seq, tokens), :], g_send.at[2 * o + b]).start()

            grads.append((2 * o + b, to))

    keep.wait()
    keeps.pop(0)
    og_load.wait()
    project(0)
    for i in range(4):
        for j in range(1, 4):
            piece = part(3, i, x_from(j))
            remote(piece, piece, wxx_send.at[i, j - 1], wxx_recv.at[i, j - 1], along_x(-j)).wait_recv()
        send_sibling(3, i, whole(3, i))
    project(1)
    project(2)
    project(3)

    for copy in keeps:
        copy.wait()
    for r in far_first:
        arrival(2, r).wait_recv()
    for n in range(2):
        for r in range(8):
            for side in range(2):
                passed(n, r, side).wait_recv()

    tiles = count_ref.shape[0]
    heads = q_buf.shape[1] // HD
    factor = HD ** -0.5
    base_tile = win_ref[0, 0] - tiles

    def place_of(t, j):
        return jnp.maximum(jnp.minimum(win_ref[t, j] - base_tile, 3 * tiles - 1), 0)

    for i in range(3 * tiles):
        for h in range(heads):
            k_tile[h, i] = k_out[i * TILE:(i + 1) * TILE, h * HD:(h + 1) * HD]
            v_tile[h, i] = v_out[i * TILE:(i + 1) * TILE, h * HD:(h + 1) * HD]

    def forward(h, t):
        cols = slice(h * HD, (h + 1) * HD)
        here = rows_of(t, TILE)
        q = q_buf[here, cols]
        top = None
        for j in range(WIN):
            scores = dotT(q, k_tile[h, place_of(t, j)])
            if j > 0:
                scores = scores + jnp.minimum(count_ref[t] - 1 - j, 0).astype(F32) * 1e30
            s_buf[j] = scores
            m = jnp.max(scores, axis=1, keepdims=True)
            top = m if top is None else jnp.maximum(top, m)
        total = jnp.zeros((TILE, 1), F32)
        acc = jnp.zeros((TILE, HD), F32)
        for j in range(WIN):
            e = jnp.exp2((s_buf[j] - top) * (factor * LOG2E))
            total = total + jnp.sum(e, axis=1, keepdims=True)
            eb = e.astype(BF16)
            e_buf[h * tiles + t, j] = eb
            acc = acc + dot(eb, v_tile[h, place_of(t, j)])
        inv = 1.0 / total
        attn = acc * inv
        attn_f[here, cols] = attn
        inv_f[here, cols] = jnp.broadcast_to(inv, (TILE, HD))
        attn_b[here, cols] = attn.astype(BF16)

    def backward(h, t):
        cols = slice(h * HD, (h + 1) * HD)
        here = rows_of(t, TILE)
        g = g_out[here, cols]
        gf = g.astype(F32)
        inv = inv_f[here, cols]
        centre = jnp.sum(gf * attn_f[here, cols], axis=1, keepdims=True)
        gs = (gf * inv).astype(BF16)
        qs = (q_buf[here, cols].astype(F32) * (inv * factor)).astype(BF16)
        dq = jnp.zeros((TILE, HD), F32)
        for j in range(WIN):
            at = place_of(t, j)
            dp_j = dotT(g, v_tile[h, at])
            eb = e_buf[h * tiles + t, j]
            ds = (eb.astype(F32) * (dp_j - centre)).astype(BF16)
            dq = dq + dot(ds, k_tile[h, at])
            pieces[0, t * WIN + j] = dot0(ds, qs)
            pieces[1, t * WIN + j] = dot0(eb, gs)
        dq_b[here, cols] = (dq * (inv * factor)).astype(BF16)

    def each_tile(what, h):
        def step(t, carry):
            what(h, t)
            return carry
        lax.fori_loop(0, tiles, step, 0)

    locals_ = []

    def local(src, dst, sem):
        copy = pltpu.make_async_copy(src, dst, sem)
        copy.start()
        locals_.append(copy)

    def head_columns(index, h):
        return pl.ds(pl.multiple_of(index * 256 + h * HD, HD), HD)

    def to_tokens(src, out, h, send, recv):
        cols = slice(h * HD, (h + 1) * HD)
        for r in far_first:
            to = ring(seq, r, 8)
            go(remote(src.at[rows_of(to, tokens), cols], out.at[:, head_columns(pair, h)], send.at[h, r], recv.at[h, r], (dp, to)))
        local(src.at[rows_of(seq, tokens), cols], out.at[:, head_columns(pair, h)], recv.at[h, 0])

    def from_heads(src, out, h, send, recv):
        for r in far_first:
            came = ring(seq, -r, 8)
            remote(src.at[rows_of(came, tokens), slice(h * HD, (h + 1) * HD)], out.at[:, head_columns(flip(dp, came), h)],
                   send.at[h, r], recv.at[h, r], (dp, came)).wait_recv()

    for h in range(heads):
        each_tile(forward, h)
        to_tokens(attn_b, tok, h, t_send, t_recv)

    for r in range(1, 8):
        src = ring(seq, -r, 8)
        remote(g_stage.at[0], g_out.at[rows_of(src, tokens), :], g_send.at[0], g_recv.at[src], (dp, src)).wait_recv()
    for slot, to in grads:

        @pl.when(to != seq)
        def _():
            remote(g_stage.at[slot], g_out.at[rows_of(seq, tokens), :], g_send.at[slot], g_recv.at[seq],
                   (dp, to)).wait_send()

        @pl.when(to == seq)
        def _():
            pltpu.make_async_copy(g_stage.at[slot], g_out.at[rows_of(seq, tokens), :], g_send.at[slot]).wait()

    empty = tiles * WIN
    for n in range(2):
        pieces[n, empty] = jnp.zeros((TILE, HD), F32)

    def found(t, tile):
        slot = empty
        for j in range(WIN):
            away = place_of(t, j) - tile
            slot = slot + (1 - jnp.minimum(away * away, 1)) * (t * WIN + j - empty)
        slot = jnp.maximum(slot, 0)
        return slot

    def fold(h):
        cols = slice(h * HD, (h + 1) * HD)

        def step(i, carry):
            here = rows_of(i, TILE)
            for place in range(3):
                slots = [found(t, place * tiles + i) for t in range(tiles)]
                for n in range(2):
                    total = pieces[n, slots[0]]
                    for slot in slots[1:]:
                        total = total + pieces[n, slot]
                    if place == 1:
                        own[n, here, cols] = total
                    else:
                        rim_buf[place // 2, n, here, cols] = total.astype(BF16)
            return carry

        lax.fori_loop(0, tiles, step, 0)

    into = (high, low)
    half = 4 * tokens

    def rim(h, n, side, part_of, device):
        at = rows_of(part_of, half)
        cols = slice(h * HD, (h + 1) * HD)
        return remote(rim_buf.at[side, n, at, cols], into[side].at[n, at, cols],
                      r_send.at[h, side * 2 + n, part_of], r_recv.at[h, side * 2 + n, part_of], device)

    for h in range(heads):
        each_tile(backward, h)
        to_tokens(dq_b, dq_out, h, d_send, d_recv)
        fold(h)
        for k in range(2):
            for side in range(2):
                first = 1 - beside[side][1] // 4
                for n in range(2):
                    go(rim(h, n, side, first if k == 0 else 1 - first, beside[side]))

    outs = (dk_out, dv_out)

    def finish(h):
        cols = slice(h * HD, (h + 1) * HD)
        for k in range(2):
            part_of = 1 - seq // 4 if k == 0 else seq // 4
            for side in range(2):
                for n in range(2):
                    rim(h, n, side, part_of, beside[1 - side]).wait_recv()
            at = rows_of(part_of, half)
            for n in range(2):
                stage[n, at, cols] = (own[n, at, cols] + low[n, at, cols].astype(F32) + high[n, at, cols].astype(F32)).astype(BF16)
            for r in (4, 3, 5, 2, 6, 1, 7):
                to = ring(seq, r, 8)

                @pl.when(to // 4 == part_of)
                def _():
                    for n in range(2):
                        summed(h, n, r, to).start()

        for n in range(2):
            local(stage.at[n, rows_of(seq, tokens), cols], outs[n].at[:, head_columns(pair, h)], s_recv.at[h, n, 0])

    def summed(h, n, r, to):
        return remote(stage.at[n, rows_of(to, tokens), slice(h * HD, (h + 1) * HD)], outs[n].at[:, head_columns(pair, h)],
                      s_send.at[h, n, r], s_recv.at[h, n, r], (dp, to))

    finish(0)
    for copy in locals_[:2]:
        copy.wait()
    for h in range(heads):
        from_heads(attn_b, tok, h, t_send, t_recv)
    cut = 512
    for c in range(o_out.shape[1] // cut):
        o_out[:, c * cut:(c + 1) * cut] = dot(tok[...], w_out[:, c * cut:(c + 1) * cut]).astype(BF16)
    finish(1)
    for copy in locals_[2:]:
        copy.wait()
    for h in range(heads):
        from_heads(dq_b, dq_out, h, d_send, d_recv)
        for r in far_first:
            came = ring(seq, -r, 8)
            for n in range(2):
                remote(stage.at[n, rows_of(came, tokens), slice(h * HD, (h + 1) * HD)],
                       outs[n].at[:, head_columns(flip(dp, came), h)], s_send.at[h, n, r], s_recv.at[h, n, r], (dp, came)).wait_recv()
                summed(h, n, r, ring(seq, r, 8)).wait_send()
    for copy in pending:
        copy.wait_send()


def body(query, key_in, value, out_weight, out_grad, windows, window_count):
    tokens, width = query.shape
    depth = out_weight.shape[1]
    tiles = windows.shape[0]
    rows = 8 * tokens
    vm = pl.BlockSpec(memory_space=pltpu.VMEM)
    sm = pl.BlockSpec(memory_space=pltpu.SMEM)
    hbm = pl.BlockSpec(memory_space=pl.ANY)
    sem = pltpu.SemaphoreType.DMA
    wide = jax.ShapeDtypeStruct((tokens, width), BF16)
    slab = (rows, 256)
    pairs = [(3, 8), (2, 2, 8), (8,), (3,), (3, 3), (2, 4), (4,), (4, 3), (16,), (2, 8), (2, 8), (2, 4, 2), (2, 2, 8)]
    scratch = [
        (slab, BF16), ((3 * rows, 256), BF16), ((3 * rows, 256), BF16), (slab, BF16), ((width, depth), BF16),
        ((tokens, depth), BF16), ((8, tokens, 256), BF16), ((WIN, TILE, TILE), F32), ((2 * tiles, WIN, TILE, TILE), BF16),
        (slab, F32), (slab, F32), (slab, BF16), (slab, BF16), ((2, tiles * WIN + 1, TILE, HD), F32), ((2,) + slab, F32),
        ((2, 3 * tiles, TILE, HD), BF16), ((2, 3 * tiles, TILE, HD), BF16), ((2, 2) + slab, BF16), ((2,) + slab, BF16), ((2,) + slab, BF16), ((2,) + slab, BF16), ((tokens, width), BF16),
    ]
    return tuple(pl.pallas_call(
        layer,
        out_shape=[jax.ShapeDtypeStruct((tokens, depth), BF16), wide, wide, wide],
        in_specs=[sm, sm] + [hbm] * 5,
        out_specs=[vm] * 4,
        scratch_shapes=[pltpu.VMEM(*p) for p in scratch]
        + [sem(p) for p in pairs for _ in range(2)] + [sem((5,))],
        compiler_params=pltpu.CompilerParams(collective_id=0, has_side_effects=True, vmem_limit_bytes=63 << 20),
    )(windows, window_count, query, key_in, value, out_weight, out_grad))


def solution(mesh):
    both = P(("dp", "seq"), None)
    return jax.shard_map(
        body, mesh=mesh, check_vma=False,
        in_specs=(both, both, both, P("dp", None), both, P("dp", None), P("dp")),
        out_specs=(both, both, both, both),
    )
```

time: 227 us -> 171 us (0.75)
  the two profiles are of different devices: /device:TPU:14 before, /device:TPU:32 now
where the time goes in v3:
time: 171 us; the launch traced here: 168 us
  Pallas kernels  162 us (95%)
  local copies, waits for them, and re-layouts  5.57 us (3%)
    pallas_call x1, Pallas kernels, body(): pl.pallas_call(layer, out_shape=[jax.ShapeDtypeStruct((tokens, depth), BF...  162 us
    unnamed x10, local copies, waits for them, and re-layouts  5.57 us

profile of v3, /device:TPU:32, one launch (start us, length us, event | category | flops | bytes accessed | tf_op | source)
XLA Modules:
  0.0 168.2 jit_solution(18282850689364415127)
XLA Ops:
  0.6 161.9 %shard_map.102 = (bf16[144,3072]{1,0:T(8,128)(2,1)}, bf16[144,2048]{1,0:T(8,128)(2,1)}, bf16[144,2048]{1,0:T(8,128)(2,1)}, bf16[144,2048]{1,0:T(8,128)(2,1)}) custom-call(s32[3,5]{1,0:T(4,128)} %win_ref.1, s32[3]{0:T(128)} %count_ref.1, bf16[144,2048]{1,0:T(8,128)(2,1)} %q_ref.1, bf16[144,2048]{1,0:T(8,128)(2,1)} %k_ref.1, bf16[144,2048]{1,0:T(8,128)(2,1)} %v_ref.1, ...), custom_call_target="tpu_custom_call" | custom-call | tf_op jit(solution)/shard_map/pallas_call | solution.py:494
  162.6 0.0 copy-start.2
  162.6 2.2 %copy.15 = bf16[144,3072]{1,0:T(8,128)(2,1)} copy(bf16[144,3072]{1,0:T(8,128)(2,1)} %get-tuple-element.8) | data formatting | bytes 1769472
  164.8 0.0 copy-done.2
  164.8 0.0 copy-start.1
  164.8 0.8 copy.16
  165.6 0.5 copy-done.1
  166.1 0.0 copy-start
  166.1 0.8 copy.17
  166.9 0.5 copy-done
  167.3 0.8 copy.18
Async XLA Ops:
  162.6 2.2 %copy-start.2 = (bf16[144,2048]{1,0:T(8,128)(2,1)S(1)}, bf16[144,2048]{1,0:T(8,128)(2,1)}, u32[]{:S(2)}) copy-start(bf16[144,2048]{1,0:T(8,128)(2,1)} %get-tuple-element.9) | copy-start | bytes 1769476
  164.8 1.3 copy-start.1
  166.1 1.3 copy-start
